TPU v7x, 128 devices: a whole 4x4x4 slice. The times are simulated.
128 devices in a mesh: blk: 8 (over y, core), row: 16 (over x, z).
Axes of the slice: x: 4, y: 4, z: 4, core: 2. Of those that a mesh axis runs over, the one named last changes fastest.
Arguments:
- factor: float32 [8, 3072, 3072], P('blk', 'row'), may hold values from -1 to 1, as said below
- coupling: float32 [8, 128, 128], P('blk'), may hold values from -1.5 to 1.5
- right_side: float32 [8, 3072, 128], P('blk', 'row'), may hold values from -6 to 6
Outputs:
- inverse: float32 [8, 3072, 3072], P('blk', 'row')
- solution: float32 [8, 3072, 128], P('blk', 'row')
Inputs may be any that keep to these rules, and one draw needn't show every extreme that they name: Each factor[b] has ones on its diagonal and zeros above it.
All inputs are finite; a program needn't handle non-finite values.
Results may differ from a plain program's by a relative error of at most 0.0003.
Values sent between devices are 32-bit elements; how exact they have to be, the bound alone decides.
A program may use at most 128 MiB of HBM per device.

v0:
```python
import jax
import jax.numpy as jnp
from jax import lax
from jax.sharding import PartitionSpec as P

highest = lax.Precision.HIGHEST


def swapped(block, axis, bit):
    count = lax.axis_size(axis)
    route = []
    for low in range(count):
        high = low | 1 << bit
        if high != low and high < count:
            route += [(low, high), (high, low)]
    return lax.ppermute(block, axis, route)


def from_behind(block, axis, distance):
    devices = range(lax.axis_size(axis))
    route = [(i - distance, i) for i in devices if i - distance in devices]
    return lax.ppermute(block, axis, route)


def joined_along(blocks, dim):
    shape = list(blocks.shape[1:])
    shape[dim] *= blocks.shape[0]
    return jnp.moveaxis(blocks, 0, dim).reshape(shape)


def sent_to_all(value, axis):
    size = lax.axis_size(axis)
    return lax.all_to_all(
        jnp.broadcast_to(value[None], (size, *value.shape)), axis, 0, 0, tiled=True
    )


def collect(value, axis, dim):
    return joined_along(sent_to_all(value, axis), dim)


def from_root(value, axis, root):
    return lax.dynamic_index_in_dim(lax.all_gather(value, axis), root, 0, keepdims=False)


def entering(value, axis, join, neutral):
    count, mine = (lax.axis_size(axis), lax.axis_index(axis))
    pieces = jax.tree.map(lambda part: lax.all_gather(part, axis), value)
    so_far = jax.tree.map(
        lambda part, zero: jnp.full_like(part, 0) + jnp.asarray(zero, part.dtype), value, neutral
    )

    def turn(position, so_far):
        longer = join(so_far, jax.tree.map(lambda part: part[position], pieces))
        return jax.tree.map(lambda new, old: jnp.where(position < mine, new, old), longer, so_far)

    return lax.fori_loop(0, count - 1, turn, so_far)


def stacked(own_rows, partner, my_index, bit_index):
    is_high = jnp.bitwise_and(jnp.right_shift(my_index, bit_index), 1) == 1
    return jnp.where(
        is_high,
        jnp.concatenate([partner, own_rows], axis=1),
        jnp.concatenate([own_rows, partner], axis=1),
    )


def unit_solve(matrix, target, transposed):
    return jax.scipy.linalg.solve_triangular(
        matrix, target, trans=transposed, lower=True, unit_diagonal=True
    )


def sweep_local(incoming, tail_gain, tail_term):
    current = incoming
    previous = [current]
    current = tail_term[0] + jnp.dot(tail_gain[0], current, precision=highest)
    return (current, jnp.stack(previous))


def compose(earlier, later):
    return (
        jnp.dot(later[0], earlier[0], precision=highest),
        jnp.dot(later[0], earlier[1], precision=highest) + later[1],
    )


def on_device(factor, coupling, right_side):
    row_count = lax.axis_size("row")
    my_index = lax.axis_index("row")
    local_blocks, panel_rows, block_order = factor.shape
    band_width = coupling.shape[1]
    levels = row_count.bit_length() - 1
    identity = jnp.eye(panel_rows, dtype=jnp.float32)
    first_col = my_index * panel_rows
    diagonal = lax.dynamic_slice_in_dim(factor, first_col, panel_rows, 2)
    base_inverse = jax.vmap(lambda matrix: unit_solve(matrix, identity, 0))(diagonal)
    inverse = lax.dynamic_update_slice_in_dim(jnp.zeros_like(factor), base_inverse, first_col, 2)
    for section_level in range(levels):
        half_size = 1 << section_level
        span_width = half_size * panel_rows
        offset = my_index % (2 * half_size)
        group_first = (my_index - offset) * panel_rows
        is_lower = offset >= half_size
        inverse_piece = lax.dynamic_slice_in_dim(inverse, group_first, span_width, 2)
        factor_piece = lax.dynamic_slice_in_dim(factor, group_first, span_width, 2)
        assembled = jnp.where(is_lower, factor_piece, inverse_piece)
        for bit_index in range(section_level):
            partner = swapped(assembled, "row", bit_index)
            assembled = stacked(assembled, partner, my_index, bit_index)
        leading = from_behind(assembled, "row", half_size)
        corner_block = lax.dynamic_slice_in_dim(inverse, group_first + span_width, span_width, 2)
        coupled = jnp.einsum("nrw,nwv->nrv", corner_block, assembled, precision=highest)
        new_rows = -jnp.einsum("nrw,nwv->nrv", coupled, leading, precision=highest)
        inverse = jnp.where(
            is_lower, lax.dynamic_update_slice_in_dim(inverse, new_rows, group_first, 2), inverse
        )
    direct = jnp.einsum("nrb,nbk->nrk", inverse, collect(right_side, "row", 1), precision=highest)
    gain_cols = -jnp.einsum("nrb,nbc->nrc", inverse[:, :, :band_width], coupling, precision=highest)
    tail_rows = jnp.concatenate(
        [gain_cols[:, panel_rows - band_width :, :], direct[:, panel_rows - band_width :, :]],
        axis=2,
    )
    tail_rows = from_root(tail_rows, "row", row_count - 1)
    tail_gain = tail_rows[:, :, :band_width]
    tail_term = tail_rows[:, :, band_width:]
    zero_tail = jnp.zeros((band_width, right_side.shape[2]), jnp.float32)
    matrix = jnp.eye(band_width, dtype=jnp.float32)
    shifted = zero_tail
    matrix, shifted = compose((matrix, shifted), (tail_gain[0], tail_term[0]))
    identity_map = (jnp.eye(band_width, dtype=jnp.float32), zero_tail)
    prefix_map = entering((matrix, shifted), "blk", compose, identity_map)
    incoming = prefix_map[1]
    final_tail, previous = sweep_local(incoming, tail_gain, tail_term)
    solution = direct + jnp.einsum("nrc,nck->nrk", gain_cols, previous, precision=highest)
    return (inverse, solution)


def solution(mesh):
    in_specs = (P("blk", "row", None), P("blk", None, None), P("blk", "row", None))
    out_specs = (P("blk", "row", None), P("blk", "row", None))
    return jax.shard_map(
        on_device, mesh=mesh, in_specs=in_specs, out_specs=out_specs, check_vma=False
    )
```

profile of v0, /device:TPU:22, one launch (start us, length us, event | category | flops | bytes accessed | tf_op | source)
XLA Modules:
  0.0 682.8 jit_solution(406792278737041890)
XLA Ops:
  7.3 1.1 convert_add_fusion
  8.5 19.7 %custom-call.4 = f32[1,2,128,128]{2,3,1,0:T(8,128)S(1)} custom-call(f32[1,2,128,128]{3,2,1,0:T(8,128)S(1)} %pad_maximum_fusion.1), custom_call_target="InvertDiagBlocksLowerTriangular" | custom-call | tf_op jit(solution)/shard_map/vmap(jit(_solve_triangular))/triangular_solve | solution.py:70
  29.6 1.5 dynamic_update_slice.2
  31.1 1.1 dynamic-slice_select_fusion.3
  32.3 4.1 collective-permute-start
  36.8 6.9 %collective-permute-done = f32[1,192,192]{2,1,0:T(8,128)S(1)} collective-permute-done((f32[1,192,192]{2,1,0:T(8,128)S(1)}, f32[1,192,192]{2,1,0:T(8,128)S(1)}, u32[]{:S(2)}, u32[]{:S(2)}) %collective-permute-start) | collective-permute-done | bytes 147488 | tf_op jit(solution)/shard_map/ppermute | solution.py:22
  44.0 1.5 select_n.300
  45.5 1.2 dynamic-slice_select_fusion.2
  46.8 8.2 %collective-permute-done.1 = f32[1,192,384]{2,1,0:T(8,128)S(1)} collective-permute-done((f32[1,192,384]{2,1,0:T(8,128)S(1)}, f32[1,192,384]{2,1,0:T(8,128)S(1)}, u32[]{:S(2)}, u32[]{:S(2)}) %collective-permute-start.1) | collective-permute-done | bytes 294944 | tf_op jit(solution)/shard_map/ppermute | solution.py:16
  56.6 2.0 collective-permute-start.2
  58.6 1.9 fusion.55
  60.5 14.2 %collective-permute-done.2 = f32[1,384,384]{2,1,0:T(8,128)S(1)} collective-permute-done((f32[1,384,384]{2,1,0:T(8,128)}, f32[1,384,384]{2,1,0:T(8,128)S(1)}, u32[]{:S(2)}, u32[]{:S(2)}) %collective-permute-start.2) | collective-permute-done | bytes 589856 | tf_op jit(solution)/shard_map/ppermute | solution.py:22
  75.4 3.3 select_n.311
  78.7 1.5 dynamic-slice_select_fusion.1
  80.8 12.1 %collective-permute-done.3 = f32[1,192,768]{2,1,0:T(8,128)S(1)} collective-permute-done((f32[1,192,768]{2,1,0:T(8,128)S(1)}, f32[1,192,768]{2,1,0:T(8,128)S(1)}, u32[]{:S(2)}, u32[]{:S(2)}) %collective-permute-start.3) | collective-permute-done | bytes 589856 | tf_op jit(solution)/shard_map/ppermute | solution.py:16
  93.8 1.1 maximum_select_fusion.10
  94.9 1.4 maximum_select_fusion.11
  96.3 24.8 %collective-permute-done.4 = f32[1,384,768]{2,1,0:T(8,128)} collective-permute-done((f32[1,384,768]{2,1,0:T(8,128)}, f32[1,384,768]{2,1,0:T(8,128)}, u32[]{:S(2)}, u32[]{:S(2)}) %collective-permute-start.4) | collective-permute-done | bytes 1179680 | tf_op jit(solution)/shard_map/ppermute | solution.py:16
  121.1 3.3 maximum_select_fusion.7
  124.3 1.5 collective-permute-start.5
  125.8 4.3 fusion.26
  130.2 45.1 %collective-permute-done.5 = f32[1,768,768]{2,1,0:T(8,128)} collective-permute-done((f32[1,768,768]{2,1,0:T(8,128)}, f32[1,768,768]{2,1,0:T(8,128)}, u32[]{:S(2)}, u32[]{:S(2)}) %collective-permute-start.5) | collective-permute-done | bytes 2359328 | tf_op jit(solution)/shard_map/ppermute | solution.py:22
  175.3 3.4 fusion.42
  178.7 5.9 select_n.326
  184.6 2.0 dynamic-slice_select_fusion
  186.6 1.5 collective-permute-start.6
  188.1 23.3 %collective-permute-done.6 = f32[1,192,1536]{2,1,0:T(8,128)S(1)} collective-permute-done((f32[1,192,1536]{2,1,0:T(8,128)S(1)}, f32[1,192,1536]{2,1,0:T(8,128)S(1)}, u32[]{:S(2)}, u32[]{:S(2)}) %collective-permute-start.6) | collective-permute-done | bytes 1179680 | tf_op jit(solution)/shard_map/ppermute | solution.py:16
  211.6 1.6 collective-permute-start.7
  213.3 47.6 %collective-permute-done.7 = f32[1,384,1536]{2,1,0:T(8,128)S(1)} collective-permute-done((f32[1,384,1536]{2,1,0:T(8,128)S(1)}, f32[1,384,1536]{2,1,0:T(8,128)S(1)}, u32[]{:S(2)}, u32[]{:S(2)}) %collective-permute-start.7) | collective-permute-done | bytes 2359328 | tf_op jit(solution)/shard_map/ppermute | solution.py:16
  260.9 2.9 maximum_select_fusion.3
  264.3 4.7 maximum_select_fusion.4
  269.0 92.4 %collective-permute-done.8 = f32[1,768,1536]{2,1,0:T(8,128)} collective-permute-done((f32[1,768,1536]{2,1,0:T(8,128)}, f32[1,768,1536]{2,1,0:T(8,128)}, u32[]{:S(2)}, u32[]{:S(2)}) %collective-permute-start.8) | collective-permute-done | bytes 4718624 | tf_op jit(solution)/shard_map/ppermute | solution.py:16
  361.5 9.6 %maximum_select_fusion.2 = f32[1,1536,1536]{2,1,0:T(8,128)} fusion(f32[1,768,1536]{2,1,0:T(8,128)S(1)} %bitcast.140, f32[1,768,1536]{2,1,0:T(8,128)} %collective-permute-done.8, pred[]{:T(512)S(6)} %eq.39), kind=kLoop, calls=%fused_computation.16 | loop fusion | flops 7077888 | bytes 18874368 | tf_op jit(solution)/shard_map/jit(_where)/select_n | solution.py:62
  371.1 1.3 collective-permute-start.9
  372.4 1.3 broadcast_in_dim.18
  373.7 11.8 %all-to-all-start = ((f32[16,1,192,128]{3,2,1,0:T(8,128)}), f32[16,1,192,128]{3,2,1,0:T(8,128)}, u32[]{:S(2)}, u32[]{:S(2)}) async-start(f32[16,1,192,128]{3,2,1,0:T(8,128)} %broadcast_in_dim.18), calls=%async_computation | async-start | bytes 3145728 | tf_op jit(solution)/shard_map/all_to_all | solution.py:33
  385.7 10.9 %fusion.8 = f32[192,1536]{1,0:T(8,128)S(1)} fusion(f32[768,1536]{1,0:T(8,128)} %copy-done.3, f32[768,1536]{1,0:T(8,128)} %bitcast.31, pred[]{:T(512)S(6)} %eq.39, f32[1,192,3072]{2,1,0:T(8,128)S(1)} %select_n.326, s32[]{:T(128)S(6)} %select_n.329), kind=kOutput, calls=%fused_computation.10 | convolution fusion | flops 5442895872 | bytes 11796485 | tf_op jit(solution)/shard_map/nrw,nwv->nrv/dot_general | solution.py:114
  396.6 184.1 %collective-permute-done.9 = f32[1,1536,1536]{2,1,0:T(8,128)} collective-permute-done((f32[1,1536,1536]{2,1,0:T(8,128)}, f32[1,1536,1536]{2,1,0:T(8,128)}, u32[]{:S(2)}, u32[]{:S(2)}) %collective-permute-start.9) | collective-permute-done | bytes 9437216 | tf_op jit(solution)/shard_map/ppermute | solution.py:22
  580.7 10.1 %fusion.23 = f32[1,192,1536]{2,1,0:T(8,128)} fusion(f32[192,1536]{1,0:T(8,128)S(1)} %fusion.8, f32[1,1536,1536]{2,1,0:T(8,128)} %collective-permute-done.9, f32[1,192,3072]{2,1,0:T(8,128)S(1)} %select_n.326, s32[]{:T(128)S(6)} %select_n.333, pred[]{:T(512)S(6)} %ge.15), kind=kOutput, calls=%fused_computation.24 | convolution fusion | flops 5436407808 | bytes 12976133 | tf_op jit(solution)/shard_map/nrw,nwv->nrv/dot_general | solution.py:115
  590.8 4.7 select_n.345
  595.6 4.3 fusion.32
  600.9 45.4 %all-gather.5.cloned.1.call-done = f32[16,128,256]{2,1,0:T(8,128)} async-done(((f32[1,128,256]{2,1,0:T(8,128)}), f32[16,128,256]{2,1,0:T(8,128)}) %all-gather.5.cloned.1.call-update) | async-done | bytes 2097168 | tf_op jit(solution)/shard_map/all_gather | solution.py:43
  646.2 1.0 fusion.75
  647.3 11.9 %all-gather.1 = f32[1024,128]{1,0:T(8,128)S(1)} all-gather(f32[128,128]{1,0:T(8,128)S(1)} %fusion.75), channel_id=3, replica_groups=mesh['blk'=8,'row'=16] {'blk'}, dimensions={0}, use_global_device_ids=true | all-gather | bytes 589824 | tf_op jit(solution)/shard_map/all_gather | solution.py:48
  659.2 1.1 convolution_add_fusion.2
  660.2 13.1 %all-gather.2 = f32[1024,128]{1,0:T(8,128)S(1)} all-gather(f32[128,128]{1,0:T(8,128)S(1)} %convolution_add_fusion.2), channel_id=4, replica_groups=mesh['blk'=8,'row'=16] {'blk'}, dimensions={0}, use_global_device_ids=true | all-gather | bytes 589824 | tf_op jit(solution)/shard_map/all_gather | solution.py:48
  673.3 1.7 while.16
  675.1 0.9 fusion.52
  (63 shorter events, 9.7 us)
Async XLA Ops:
  7.2 592.7 %copy-start = (f32[1,128,128]{2,1,0:T(8,128)S(1)}, f32[1,128,128]{2,1,0:T(8,128)}, u32[]{:S(2)}) copy-start(f32[1,128,128]{2,1,0:T(8,128)} %param.6) | copy-start | bytes 196612
  32.3 11.4 %collective-permute-start = (f32[1,192,192]{2,1,0:T(8,128)S(1)}, f32[1,192,192]{2,1,0:T(8,128)S(1)}, u32[]{:S(2)}, u32[]{:S(2)}) collective-permute-start(f32[1,192,192]{2,1,0:T(8,128)S(1)} %dynamic-slice_select_fusion.3), channel_id=1, source_target_pairs={{0,1},{1,2},{2,3},{3,4},{4,5},{5,6},{6,7},{7,8},{8,9},{9,10},{10,1... | collective-permute-start | bytes 442376 | tf_op jit(solution)/shard_map/ppermute | solution.py:22
  46.7 8.3 %collective-permute-start.1 = (f32[1,192,384]{2,1,0:T(8,128)S(1)}, f32[1,192,384]{2,1,0:T(8,128)S(1)}, u32[]{:S(2)}, u32[]{:S(2)}) collective-permute-start(f32[1,192,384]{2,1,0:T(8,128)S(1)} %dynamic-slice_select_fusion.2), channel_id=1, source_target_pairs={{0,1},{1,0},{2,3},{3,2},{4,5},{5,4},{6,7},{7,6},{8,9},{9,8},{10,11... | collective-permute-start | bytes 884744 | tf_op jit(solution)/shard_map/ppermute | solution.py:16
  55.0 0.7 copy-start.7
  56.6 18.1 %collective-permute-start.2 = (f32[1,384,384]{2,1,0:T(8,128)}, f32[1,384,384]{2,1,0:T(8,128)S(1)}, u32[]{:S(2)}, u32[]{:S(2)}) collective-permute-start(f32[1,384,384]{2,1,0:T(8,128)} %maximum_select_fusion.14), channel_id=1, source_target_pairs={{0,2},{1,3},{2,4},{3,5},{4,6},{5,7},{6,8},{7,9},{8,10},{9,11},{10,... | collective-permute-start | bytes 1769480 | tf_op jit(solution)/shard_map/ppermute | solution.py:22
  80.2 12.8 %collective-permute-start.3 = (f32[1,192,768]{2,1,0:T(8,128)S(1)}, f32[1,192,768]{2,1,0:T(8,128)S(1)}, u32[]{:S(2)}, u32[]{:S(2)}) collective-permute-start(f32[1,192,768]{2,1,0:T(8,128)S(1)} %dynamic-slice_select_fusion.1), channel_id=1, source_target_pairs={{0,1},{1,0},{2,3},{3,2},{4,5},{5,4},{6,7},{7,6},{8,9},{9,8},{10,11... | collective-permute-start | bytes 1769480 | tf_op jit(solution)/shard_map/ppermute | solution.py:16
  92.9 0.8 copy-start.6
  94.9 26.2 %collective-permute-start.4 = (f32[1,384,768]{2,1,0:T(8,128)}, f32[1,384,768]{2,1,0:T(8,128)}, u32[]{:S(2)}, u32[]{:S(2)}) collective-permute-start(f32[1,384,768]{2,1,0:T(8,128)} %maximum_select_fusion.10), channel_id=1, source_target_pairs={{0,2},{2,0},{1,3},{3,1},{4,6},{6,4},{5,7},{7,5},{8,10},{10,8},{9,1... | collective-permute-start | bytes 3538952 | tf_op jit(solution)/shard_map/ppermute | solution.py:16
  96.3 28.0 %copy-start.5 = (f32[384,768]{1,0:T(8,128)}, f32[384,768]{1,0:T(8,128)S(1)}, u32[]{:S(2)}) copy-start(f32[384,768]{1,0:T(8,128)S(1)} %maximum_select_fusion.11) | copy-start | bytes 3538948
  124.3 50.9 %collective-permute-start.5 = (f32[1,768,768]{2,1,0:T(8,128)}, f32[1,768,768]{2,1,0:T(8,128)}, u32[]{:S(2)}, u32[]{:S(2)}) collective-permute-start(f32[1,768,768]{2,1,0:T(8,128)} %maximum_select_fusion.7), channel_id=1, source_target_pairs={{0,4},{1,5},{2,6},{3,7},{4,8},{5,9},{6,10},{7,11},{8,12},{9,13},{1... | collective-permute-start | bytes 7077896 | tf_op jit(solution)/shard_map/ppermute | solution.py:22
  186.6 24.8 %collective-permute-start.6 = (f32[1,192,1536]{2,1,0:T(8,128)S(1)}, f32[1,192,1536]{2,1,0:T(8,128)S(1)}, u32[]{:S(2)}, u32[]{:S(2)}) collective-permute-start(f32[1,192,1536]{2,1,0:T(8,128)S(1)} %dynamic-slice_select_fusion), channel_id=1, source_target_pairs={{0,1},{1,0},{2,3},{3,2},{4,5},{5,4},{6,7},{7,6},{8,9},{9,8},{10,11... | collective-permute-start | bytes 3538952 | tf_op jit(solution)/shard_map/ppermute | solution.py:16
  211.6 49.3 %collective-permute-start.7 = (f32[1,384,1536]{2,1,0:T(8,128)S(1)}, f32[1,384,1536]{2,1,0:T(8,128)S(1)}, u32[]{:S(2)}, u32[]{:S(2)}) collective-permute-start(f32[1,384,1536]{2,1,0:T(8,128)S(1)} %maximum_select_fusion.8), channel_id=1, source_target_pairs={{0,2},{2,0},{1,3},{3,1},{4,6},{6,4},{5,7},{7,5},{8,10},{10,8},{9,1... | collective-permute-start | bytes 7077896 | tf_op jit(solution)/shard_map/ppermute | solution.py:16
  213.3 50.4 %copy-start.2 = (f32[384,1536]{1,0:T(8,128)}, f32[384,1536]{1,0:T(8,128)S(1)}, u32[]{:S(2)}) copy-start(f32[384,1536]{1,0:T(8,128)S(1)} %maximum_select_fusion.9) | copy-start | bytes 7077892
  260.9 2.9 copy-start.4
  263.8 97.7 %collective-permute-start.8 = (f32[1,768,1536]{2,1,0:T(8,128)}, f32[1,768,1536]{2,1,0:T(8,128)}, u32[]{:S(2)}, u32[]{:S(2)}) collective-permute-start(f32[1,768,1536]{2,1,0:T(8,128)} %maximum_select_fusion.3), channel_id=1, source_target_pairs={{0,4},{4,0},{1,5},{5,1},{2,6},{6,2},{3,7},{7,3},{8,12},{12,8},{9,1... | collective-permute-start | bytes 14155784 | tf_op jit(solution)/shard_map/ppermute | solution.py:16
  269.0 102.1 %copy-start.3 = (f32[768,1536]{1,0:T(8,128)}, f32[768,1536]{1,0:T(8,128)S(1)}, u32[]{:S(2)}) copy-start(f32[768,1536]{1,0:T(8,128)S(1)} %maximum_select_fusion.4) | copy-start | bytes 14155780
  361.5 10.9 %copy-start.8 = (f32[1,192,128]{2,1,0:T(8,128)S(1)}, f32[1,192,128]{2,1,0:T(8,128)}, u32[]{:S(2)}) copy-start(f32[1,192,128]{2,1,0:T(8,128)} %param.7) | copy-start | bytes 294916
  371.1 209.6 %collective-permute-start.9 = (f32[1,1536,1536]{2,1,0:T(8,128)}, f32[1,1536,1536]{2,1,0:T(8,128)}, u32[]{:S(2)}, u32[]{:S(2)}) collective-permute-start(f32[1,1536,1536]{2,1,0:T(8,128)} %maximum_select_fusion.2), channel_id=1, source_target_pairs={{0,8},{1,9},{2,10},{3,11},{4,12},{5,13},{6,14},{7,15},{16,24},{17,... | collective-permute-start | bytes 28311560 | tf_op jit(solution)/shard_map/ppermute | solution.py:22
  373.7 221.8 %all-to-all-start = ((f32[16,1,192,128]{3,2,1,0:T(8,128)}), f32[16,1,192,128]{3,2,1,0:T(8,128)}, u32[]{:S(2)}, u32[]{:S(2)}) async-start(f32[16,1,192,128]{3,2,1,0:T(8,128)} %broadcast_in_dim.18), calls=%async_computation | async-start | bytes 3145728 | tf_op jit(solution)/shard_map/all_to_all | solution.py:33
  385.5 260.8 %all-gather.5.cloned.1.call-start = ((), (), s32[]{:S(2)}) async-start(), calls=%async_computation.1 | async-start | bytes 2228224 | tf_op jit(solution)/shard_map/all_gather | solution.py:43
  595.5 5.3 copy-start.1
Sparse Core Ops, SparseCore 0:
  601.0 45.2 all-gather.4
where the time goes:
time: 687 us; the launch traced here: 683 us
  waiting for transfers between devices  504 us (73%)
  other arithmetic  51.7 us (8%)
  matrix products  41.8 us (6%)
  starting transfers between devices  25.2 us (4%)
  blocking collectives  25 us (4%)
  local copies, waits for them, and re-layouts  20.2 us (3%)
  between operations  14.6 us (2%)
    ppermute x4, waiting for transfers between devices, from_behind(): return lax.ppermute(block, axis, route)  250 us
    ppermute x6, waiting for transfers between devices, swapped(): return lax.ppermute(block, axis, route)  208 us
    all_gather x1, waiting for transfers between devices, from_root(): lax.all_gather(value, axis)  45.4 us
    all_gather x2, blocking collectives, entering(): pieces = jax.tree.map(lambda part: lax.all_gather(part, axis), value)  25 us
    select_n x9, other arithmetic, stacked(): jnp.where(is_high, jnp.concatenate([partner, own_rows], axis=1), jnp.conc...  24.3 us
    another operation x8, other arithmetic, unit_solve(): jax.scipy.linalg.solve_triangular(matrix, target, trans=transposed, lower...  20.9 us
    dot_general x4, matrix products, on_device(): jnp.einsum('nrw,nwv->nrv', corner_block, assembled, precision=highest)  17.4 us
    select_n x4, local copies, waits for them, and re-layouts, on_device(): jnp.where(is_lower, lax.dynamic_update_slice_in_dim(inverse, new_rows, gr...  15.4 us
  transfers between devices with their start and end apart: 12, of which 11 were waited for; matrix products, arithmetic and copies ran while one was open for 6% of the time, Pallas kernels for 0%

commit v1 on v0

v1 whole, which is shorter than its diff:
```python
import functools

import jax
import jax.numpy as jnp
from jax import lax
from jax.experimental import pallas as pl
from jax.experimental.pallas import tpu as pltpu
from jax.sharding import PartitionSpec as P

MESH = pl.DeviceIdType.MESH
RING = 4
TARGETS = {0: (3, 1, 2), 1: (0, 2), 2: (3,), 3: ()}
RELAYED = {1: (3,)}


def dot(a, b):
    return jnp.dot(a, b, precision=lax.Precision.HIGHEST, preferred_element_type=jnp.float32)


def unit_lower_inverse(matrix):
    size = matrix.shape[0]
    rows = lax.broadcasted_iota(jnp.int32, (size, size), 0)
    cols = lax.broadcasted_iota(jnp.int32, (size, size), 1)
    inverse = jnp.where(rows == cols, 1.0, 0.0).astype(jnp.float32)
    bit = 0
    while (1 << bit) < size:
        same = (rows >> (bit + 1)) == (cols >> (bit + 1))
        corner = same & (((rows >> bit) & 1) == 1) & (((cols >> bit) & 1) == 0)
        below = jnp.where(corner, matrix, 0.0)
        if bit == 0:
            inverse = inverse - below
        else:
            inverse = inverse - dot(dot(inverse, below), inverse)
        bit += 1
    return inverse


class Copies:
    def __init__(self, sems):
        self.sems, self.used, self.ends = sems, 0, []

    def slot(self):
        self.used += 1
        return self.used - 1

    def remote(self, when, source, target, arrival, device, slot=None):
        sem = self.sems.at[self.slot() if slot is None else slot]

        def make():
            return pltpu.make_async_remote_copy(
                src_ref=source,
                dst_ref=target,
                send_sem=sem,
                recv_sem=arrival,
                device_id=device,
                device_id_type=MESH,
            )

        pl.when(when)(lambda: make().start())
        self.ends.append((when, lambda: make().wait_send()))

    def local(self, when, source, target, sem, waited=True):
        pl.when(when)(lambda: pltpu.make_async_copy(source, target, sem).start())
        if waited:
            self.ends.append((when, lambda: pltpu.make_async_copy(source, target, sem).wait()))

    def finish(self):
        for when, end in self.ends:
            pl.when(when)(end)


def arrived(when, target, sem):
    pl.when(when)(lambda: pltpu.make_async_copy(target, target, sem).wait())


def solve_kernel(pairs, fac, diag, corner, rhs, inv, direct, *scratch):
    lbuf = (None, *scratch[: pairs - 1])
    ebuf, own, xa, dinv, dleft, dloc, sends, rl, re, rx, rd, lx = scratch[pairs - 1 :]
    size = fac.shape[0]
    half, wide = size // 2, 2 * size
    blk, row = lax.axis_index("blk"), lax.axis_index("row")
    core = lax.rem(blk, 2)
    x, z = lax.div(row, RING), lax.rem(row, RING)
    zhi, odd = lax.div(z, 2), lax.rem(z, 2)
    mine = 2 * x + zhi
    home = core == 1 - odd
    away = core == odd
    first = blk - core

    def at(to_x, to_z, to_core):
        return {"blk": first + to_core, "row": to_x * RING + to_z}

    def aligned(index, by):
        return pl.multiple_of(index, by)

    barrier = pltpu.get_barrier_semaphore()
    peers = [(x, z, 1 - core)]
    for step in range(1, RING):
        for side in range(2):
            peers += [(x, lax.rem(z + step, RING), side), (lax.rem(x + step, RING), z, side)]
    for peer in peers:
        pl.semaphore_signal(barrier, inc=1, device_id=at(*peer), device_id_type=MESH)
    pl.semaphore_wait(barrier, len(peers))

    copies = Copies(sends)

    def spread(when, source, target, arrival, rows_x, wanted, slots):
        slot = iter(slots)
        for side in range(2):
            src, dst, sem = source(side), target(side), arrival.at[row, side]
            copies.local(when & home, src, dst, sem, waited=False)
            copies.remote(when & home, src, dst, sem, at(x, z, 1 - core), next(slot))
            for r, wx in rows_x:
                for number, to_x in enumerate(TARGETS[r]):
                    copies.remote(
                        when & wx & home, src, dst, sem, at(to_x, z, side), slots[8 + 2 * number + side]
                    )
            across = lax.rem(z + 2, RING)
            copies.remote(
                when & home & wanted(across), src, dst, sem, at(x, across, side), next(slot)
            )
            for step in (1, 3):
                to_z = lax.rem(z + step, RING)
                copies.remote(
                    when & away & wanted(to_z), src, dst, sem, at(x, to_z, side), next(slot)
                )

    def wanted(to_z):
        return (x < RING - 1) | (zhi == 0) | (lax.div(to_z, 2) == 1)

    slots = [copies.slot() for _ in range(14)]
    for m in range(1, pairs):
        spread(
            mine == m,
            lambda side, m=m: fac.at[pl.ds(side * half, half), pl.ds(0, wide * m)],
            lambda side, m=m: lbuf[m].at[pl.ds(aligned(odd * size + side * half, 8), half), :],
            rl,
            [(m // 2, x == m // 2)],
            wanted,
            slots,
        )

    xa[...] = jnp.zeros_like(xa)
    inverse = unit_lower_inverse(diag[...])
    dinv[...] = inverse
    beside = at(x, z + 1 - 2 * odd, core)
    copies.remote(odd == 0, dinv, dleft, rd, beside)
    r_ids = lax.broadcasted_iota(jnp.int32, (size, wide), 0)
    c_ids = lax.broadcasted_iota(jnp.int32, (size, wide), 1)
    place = jnp.where(c_ids == r_ids + odd * size, 1.0, 0.0).astype(jnp.float32)
    own[:, pl.ds(0, wide)] = dot(inverse, place)
    own[:, pl.ds(wide, rhs.shape[1])] = rhs[...]

    @pl.when(odd == 1)
    def _():
        pltpu.make_async_copy(dleft, dleft, rd).wait()
        left = dot(dinv[...], dot(corner[...], dleft[...]))
        lead = jnp.where(c_ids == r_ids, 1.0, 0.0).astype(jnp.float32)
        own[:, pl.ds(0, wide)] = own[:, pl.ds(0, wide)] - dot(left, lead)

    slots = [copies.slot() for _ in range(14)]
    spread(
        mine >= 0,
        lambda side: own.at[pl.ds(side * half, half), :],
        lambda side: ebuf.at[pl.ds(aligned(row * size + side * half, 8), half), :],
        re,
        [(r, x == r) for r in range(RING)],
        wanted,
        slots,
    )

    def view(kind, j, side):
        if kind == "left":
            return lbuf[j // 2].at[pl.ds(aligned((j % 2) * size + side * half, 8), half), :]
        return ebuf.at[pl.ds(aligned(j * size + side * half, 8), half), :]

    def sem_of(kind, j, side):
        return (rl if kind == "left" else re).at[j, side]

    def panels(kind, numbers):
        return [j for j in numbers if kind == "right" or j >= 2]

    def forward(kind, j, when, targets, beside_too):
        here, sem = view(kind, j, core), sem_of(kind, j, core)
        arrived(when, here, sem)
        for to_x in targets:
            copies.remote(when, here, here, sem, at(to_x, z, core))
        if beside_too is not None:
            copies.remote(when & beside_too, here, here, sem, at(x, z, 1 - core))

    for kind in ("left", "right"):
        for r in range(RING):
            for j in panels(kind, range(RING * r, RING * (r + 1))):
                when = (x == r) & (z != j % RING)
                if r == RING - 1 and j % RING >= 2:
                    when = when & (zhi == 1)
                forward(kind, j, when, TARGETS[r], mine >= j // 2)
    for kind in ("left", "right"):
        for r, targets in RELAYED.items():
            for j in panels(kind, range(RING * r, RING * (r + 1))):
                forward(kind, j, x == 0, targets, None)

    def take(m):
        for kind in ("left", "right"):
            for j in panels(kind, (2 * m, 2 * m + 1)):
                forward(kind, j, x > m // 2, (), mine >= 0)

    partner = at(x, z + 1 - 2 * odd, 1 - core)
    half_of_pair = jnp.where(home, odd, 1 - odd)

    def solve(m):
        here = mine >= m
        for kind in ("left", "right"):
            for j in panels(kind, (2 * m, 2 * m + 1)):
                arrived(row == j, view(kind, j, core), sem_of(kind, j, core))
                arrived(here, view(kind, j, 1 - core), sem_of(kind, j, 1 - core))
        block = xa.at[:, pl.ds(m * wide, wide)]

        @pl.when(mine == m)
        def _():
            block[...] = ebuf[pl.ds(aligned(m * wide + half_of_pair * size, 8), size), pl.ds(0, wide)]

        @pl.when(mine > m)
        def _():
            block[...] = dot(block[...], ebuf[pl.ds(m * wide, wide), pl.ds(0, wide)])

        @pl.when(here)
        def _():
            dloc[...] += dot(block[...], ebuf[pl.ds(m * wide, wide), pl.ds(wide, dloc.shape[1])])

        if m:

            @pl.when(here)
            def _():
                @pl.loop(0, m)
                def _(n):
                    cols = pl.ds(pl.multiple_of(n * wide, wide), wide)
                    xa[:, cols] -= dot(block[...], lbuf[m][:, cols])

        result = inv.at[:, pl.ds(m * wide, wide)]
        copies.local((mine < m) | home, block, result, lx.at[m])
        copies.remote(here & away, block, result, rx.at[m], partner)

    dloc[...] = jnp.zeros_like(dloc)
    for m in reversed(range(pairs)):
        solve(m)
        if 2 <= m:
            take(m - 2)
    copies.local(home, dloc, direct, lx.at[pairs])
    copies.remote(away, dloc, direct, rx.at[pairs], partner)

    for m in range(pairs):
        arrived(away & (mine >= m), inv.at[:, pl.ds(m * wide, wide)], rx.at[m])
    arrived(away, direct, rx.at[pairs])
    copies.finish()


def invert(factor, right_side):
    size, order = factor.shape
    columns = right_side.shape[1]
    pairs, wide = order // (2 * size), 2 * size
    row = lax.axis_index("row")
    diag = lax.dynamic_slice_in_dim(factor, row * size, size, 1)
    corner = lax.dynamic_slice_in_dim(factor, (row - row % 2) * size, size, 1)
    vmem = pl.BlockSpec(memory_space=pltpu.VMEM)
    hbm = pl.BlockSpec(memory_space=pl.ANY)
    dma = pltpu.SemaphoreType.DMA
    panels = 2 * pairs
    return pl.pallas_call(
        functools.partial(solve_kernel, pairs),
        out_shape=(
            jax.ShapeDtypeStruct((size, order), jnp.float32),
            jax.ShapeDtypeStruct((size, columns), jnp.float32),
        ),
        in_specs=[vmem] * 4,
        out_specs=(hbm, hbm),
        scratch_shapes=[
            *[pltpu.VMEM((wide, wide * m), jnp.float32) for m in range(1, pairs)],
            pltpu.VMEM((order, wide + columns), jnp.float32),
            pltpu.VMEM((size, wide + columns), jnp.float32),
            pltpu.VMEM((size, order), jnp.float32),
            pltpu.VMEM((size, size), jnp.float32),
            pltpu.VMEM((size, size), jnp.float32),
            pltpu.VMEM((size, columns), jnp.float32),
            dma((200,)),
            dma((panels, 2)),
            dma((panels, 2)),
            dma((pairs + 1,)),
            dma,
            dma((pairs + 1,)),
        ],
        compiler_params=pltpu.CompilerParams(
            collective_id=0, has_side_effects=True, vmem_limit_bytes=52 * 1024 * 1024
        ),
    )(factor, diag, corner, right_side)


def tail_kernel(inv, direct, coupling, out, lead, gain, mapped, maps, tail, sends, rm, rt, lsem):
    size, width = lead.shape
    blocks, rows = maps.shape[0], lax.axis_size("row")
    blk, row = lax.axis_index("blk"), lax.axis_index("row")
    last = row == rows - 1
    barrier = pltpu.get_barrier_semaphore()

    def greet(when, device):
        def _():
            pl.semaphore_signal(barrier, inc=1, device_id=device, device_id_type=MESH)

        pl.when(when)(_)

    others = [{"blk": lax.rem(blk + step, blocks), "row": row} for step in range(1, blocks)]
    along = [{"blk": blk, "row": number} for number in range(rows - 1)]
    for device in others + along:
        greet(last, device)
    greet(row != rows - 1, {"blk": blk, "row": rows - 1})
    pl.when(last)(lambda: pl.semaphore_wait(barrier, blocks + rows - 2))
    pl.when(row != rows - 1)(lambda: pl.semaphore_wait(barrier, 1))

    copies = Copies(sends)
    fetch = pltpu.make_async_copy(inv.at[:, pl.ds(0, width)], lead, lsem)
    fetch.start()
    fetch.wait()
    gain[...] = -dot(lead[...], coupling[...])

    @pl.when(last | (blk == 0))
    def _():
        tail[...] = jnp.zeros_like(tail)

    @pl.when(last)
    def _():
        mapped[:, pl.ds(0, width)] = gain[pl.ds(size - width, width), :]
        mapped[:, pl.ds(width, direct.shape[1])] = direct[pl.ds(size - width, width), :]

    for step in range(1, blocks):
        copies.remote(
            last & (blk + step < blocks),
            mapped,
            maps.at[blk],
            rm.at[blk],
            {"blk": lax.rem(blk + step, blocks), "row": row},
        )
    for k in range(blocks - 1):

        @pl.when(last & (blk > k))
        def _():
            pltpu.make_async_copy(maps.at[k], maps.at[k], rm.at[k]).wait()
            tail[...] = (
                dot(maps[k, :, pl.ds(0, width)], tail[...])
                + maps[k, :, pl.ds(width, tail.shape[1])]
            )

    for device in along:
        copies.remote(last & (blk > 0), tail, tail, rt, device)
    arrived((row != rows - 1) & (blk > 0), tail, rt)
    out[...] = direct[...] + dot(gain[...], tail[...])
    copies.finish()


def chain(inverse, direct, coupling):
    size, columns = direct.shape
    width = coupling.shape[0]
    blocks, rows = lax.axis_size("blk"), lax.axis_size("row")
    vmem = pl.BlockSpec(memory_space=pltpu.VMEM)
    dma = pltpu.SemaphoreType.DMA
    return pl.pallas_call(
        tail_kernel,
        out_shape=jax.ShapeDtypeStruct((size, columns), jnp.float32),
        in_specs=[pl.BlockSpec(memory_space=pl.ANY), vmem, vmem],
        out_specs=vmem,
        scratch_shapes=[
            pltpu.VMEM((size, width), jnp.float32),
            pltpu.VMEM((size, width), jnp.float32),
            pltpu.VMEM((width, width + columns), jnp.float32),
            pltpu.VMEM((blocks, width, width + columns), jnp.float32),
            pltpu.VMEM((width, columns), jnp.float32),
            dma((blocks + rows,)),
            dma((blocks,)),
            dma,
            dma,
        ],
        compiler_params=pltpu.CompilerParams(
            collective_id=1, has_side_effects=True, vmem_limit_bytes=16 * 1024 * 1024
        ),
    )(inverse, direct, coupling)


def on_device(factor, coupling, right_side):
    inverse, direct = invert(factor[0], right_side[0])
    return inverse[None], chain(inverse, direct, coupling[0])[None]


def solution(mesh):
    in_specs = (P("blk", "row", None), P("blk", None, None), P("blk", "row", None))
    out_specs = (P("blk", "row", None), P("blk", "row", None))
    return jax.shard_map(
        on_device, mesh=mesh, in_specs=in_specs, out_specs=out_specs, check_vma=False
    )
```

time: 687 us -> 172 us (0.25)
  the two profiles are of different devices: /device:TPU:22 before, /device:TPU:29 now
where the time goes in v1:
time: 172 us
  Pallas kernels  165 us (96%)
  local copies, waits for them, and re-layouts  5.85 us (3%)
    pallas_call x1, Pallas kernels, invert(): pl.pallas_call(functools.partial(solve_kernel, pairs), out_shape=(jax.Sha...  95.4 us
    pallas_call x1, Pallas kernels, chain(): pl.pallas_call(tail_kernel, out_shape=jax.ShapeDtypeStruct((size, columns...  70.1 us
    unnamed x10, local copies, waits for them, and re-layouts  4.6 us

profile of v1, /device:TPU:29, one launch (start us, length us, event | category | flops | bytes accessed | tf_op | source)
XLA Modules:
  0.0 172.1 jit_solution(6091713704980579363)
XLA Ops:
  0.6 0.0 copy-start.3
  0.7 1.2 dynamic-slice_bitcast_fusion
  1.9 0.0 copy-start.2
  1.9 0.9 copy-done.2
  2.8 95.4 %shard_map.50 = (f32[192,3072]{1,0:T(8,128)}, f32[192,128]{1,0:T(8,128)S(1)}) custom-call(f32[192,3072]{1,0:T(8,128)} %bitcast.13, f32[192,192]{1,0:T(8,128)S(1)} %get-tuple-element.7.diag, f32[192,192]{1,0:T(8,128)S(1)} %get-tuple-element.6.corner, f32[192,128]{1,0:T(8,128)S(1)} %bitcast.11), custom_call_target="tpu_custom_call" | custom-call | tf_op jit(solution)/shard_map/pallas_call | solution.py:269
  98.2 0.0 copy-done.3
  98.2 0.0 copy-start
  98.3 1.7 copy-done
  99.9 0.0 copy-start.1
  99.9 70.1 %shard_map.51 = f32[192,128]{1,0:T(8,128)S(1)} custom-call(f32[192,3072]{1,0:T(8,128)S(1)} %copy-done, f32[192,128]{1,0:T(8,128)S(1)} %get-tuple-element.5.direct, f32[128,128]{1,0:T(8,128)S(1)} %bitcast.12), custom_call_target="tpu_custom_call" | custom-call | tf_op jit(solution)/shard_map/pallas_call | solution.py:365
  170.0 0.0 copy-done.1
  170.0 1.4 copy.7
  171.4 0.6 copy.8
Async XLA Ops:
  0.6 97.6 %copy-start.3 = (f32[1,128,128]{2,1,0:T(8,128)S(1)}, f32[1,128,128]{2,1,0:T(8,128)}, u32[]{:S(2)}) copy-start(f32[1,128,128]{2,1,0:T(8,128)} %param.4) | copy-start | bytes 196612
  1.9 0.9 copy-start.2
  98.2 1.7 copy-start
  99.9 70.1 %copy-start.1 = (f32[192,3072]{1,0:T(8,128)S(1)}, f32[192,3072]{1,0:T(8,128)}, u32[]{:S(2)}) copy-start(f32[192,3072]{1,0:T(8,128)} %get-tuple-element.4.inv) | copy-start | bytes 7077892

commit v2 on v1

--- a/solution.py
+++ b/solution.py
@@ -15,6 +15,20 @@
 
 def dot(a, b):
     return jnp.dot(a, b, precision=lax.Precision.HIGHEST, preferred_element_type=jnp.float32)
+
+
+def split(a):
+    high = a.astype(jnp.bfloat16)
+    return high, (a - high.astype(jnp.float32)).astype(jnp.bfloat16)
+
+
+def dot3(a, b):
+    (a_high, a_low), (b_high, b_low) = a, b
+
+    def one(p, q):
+        return jnp.dot(p, q, preferred_element_type=jnp.float32)
+
+    return one(a_high, b_high) + (one(a_high, b_low) + one(a_low, b_high))
 
 
 def unit_lower_inverse(matrix):
@@ -37,45 +51,53 @@
 
 class Copies:
     def __init__(self, sems):
-        self.sems, self.used, self.ends = sems, 0, []
+        self.sems, self.used, self.groups, self.depth, self.ending = sems, 0, [], 0, False
 
     def slot(self):
         self.used += 1
         return self.used - 1
 
-    def remote(self, when, source, target, arrival, device, slot=None):
-        sem = self.sems.at[self.slot() if slot is None else slot]
-
-        def make():
-            return pltpu.make_async_remote_copy(
-                src_ref=source,
-                dst_ref=target,
-                send_sem=sem,
-                recv_sem=arrival,
-                device_id=device,
-                device_id_type=MESH,
-            )
-
-        pl.when(when)(lambda: make().start())
-        self.ends.append((when, lambda: make().wait_send()))
-
-    def local(self, when, source, target, sem, waited=True):
-        pl.when(when)(lambda: pltpu.make_async_copy(source, target, sem).start())
-        if waited:
-            self.ends.append((when, lambda: pltpu.make_async_copy(source, target, sem).wait()))
+    def group(self, when, body):
+        if not self.depth and not self.ending:
+            self.groups.append((when, body, self.used))
+        self.depth += 1
+        pl.when(when)(lambda: body())
+        self.depth -= 1
+
+    def arrived(self, target, sem):
+        if not self.ending:
+            pltpu.make_async_copy(target, target, sem).wait()
+
+    def remote(self, source, target, arrival, device, slot=None):
+        copy = pltpu.make_async_remote_copy(
+            src_ref=source,
+            dst_ref=target,
+            send_sem=self.sems.at[self.slot() if slot is None else slot],
+            recv_sem=arrival,
+            device_id=device,
+            device_id_type=MESH,
+        )
+        if self.ending:
+            copy.wait_send()
+        else:
+            copy.start()
+
+    def local(self, source, target, sem, waited=True):
+        copy = pltpu.make_async_copy(source, target, sem)
+        if not self.ending:
+            copy.start()
+        elif waited:
+            copy.wait()
 
     def finish(self):
-        for when, end in self.ends:
-            pl.when(when)(end)
-
-
-def arrived(when, target, sem):
-    pl.when(when)(lambda: pltpu.make_async_copy(target, target, sem).wait())
+        self.ending = True
+        for when, body, self.used in self.groups:
+            self.group(when, body)
 
 
 def solve_kernel(pairs, fac, diag, corner, rhs, inv, direct, *scratch):
     lbuf = (None, *scratch[: pairs - 1])
-    ebuf, own, xa, dinv, dleft, dloc, sends, rl, re, rx, rd, lx = scratch[pairs - 1 :]
+    ebuf, own, xa, dinv, dleft, dloc, parts, sends, rl, re, rx, rd, lx = scratch[pairs - 1 :]
     size = fac.shape[0]
     half, wide = size // 2, 2 * size
     blk, row = lax.axis_index("blk"), lax.axis_index("row")
@@ -100,55 +122,86 @@
             peers += [(x, lax.rem(z + step, RING), side), (lax.rem(x + step, RING), z, side)]
     for peer in peers:
         pl.semaphore_signal(barrier, inc=1, device_id=at(*peer), device_id_type=MESH)
+
+    xa[...] = jnp.zeros_like(xa)
+    dloc[...] = jnp.zeros_like(dloc)
+    dinv[...] = unit_lower_inverse(diag[...])
     pl.semaphore_wait(barrier, len(peers))
 
     copies = Copies(sends)
-
-    def spread(when, source, target, arrival, rows_x, wanted, slots):
-        slot = iter(slots)
-        for side in range(2):
-            src, dst, sem = source(side), target(side), arrival.at[row, side]
-            copies.local(when & home, src, dst, sem, waited=False)
-            copies.remote(when & home, src, dst, sem, at(x, z, 1 - core), next(slot))
-            for r, wx in rows_x:
-                for number, to_x in enumerate(TARGETS[r]):
-                    copies.remote(
-                        when & wx & home, src, dst, sem, at(to_x, z, side), slots[8 + 2 * number + side]
-                    )
-            across = lax.rem(z + 2, RING)
-            copies.remote(
-                when & home & wanted(across), src, dst, sem, at(x, across, side), next(slot)
-            )
-            for step in (1, 3):
-                to_z = lax.rem(z + step, RING)
+    beside = at(x, z + 1 - 2 * odd, core)
+    copies.group(odd == 0, lambda: copies.remote(dinv, dleft, rd, beside))
+
+    def near(source, target, arrival, slots):
+        sides = [(source(side), target(side), arrival.at[row, side], side) for side in range(2)]
+
+        def at_home():
+            for src, dst, sem, side in sides:
+                copies.remote(src, dst, sem, at(x, z, 1 - core), slots[side])
+                copies.local(src, dst, sem, waited=False)
+
+        def along(targets):
+            for number, to_x in enumerate(targets):
+                for src, dst, sem, side in sides:
+                    copies.remote(src, dst, sem, at(to_x, z, side), slots[2 * number + 2 + side])
+
+        copies.group(home, at_home)
+        for r, targets in TARGETS.items():
+            if targets:
+                copies.group(home & (x == r), functools.partial(along, targets))
+        for number, step in enumerate((1, 3)):
+            to_z = lax.rem(z + step, RING)
+
+            def beside(number=number, to_z=to_z):
+                for src, dst, sem, side in sides:
+                    copies.remote(src, dst, sem, at(x, to_z, side), slots[2 * number + side])
+
+            copies.group(away & wanted(to_z), beside)
+
+    def far(source, target, arrival, slots):
+        to_z = lax.rem(z + 2, RING)
+
+        def across():
+            for side in range(2):
                 copies.remote(
-                    when & away & wanted(to_z), src, dst, sem, at(x, to_z, side), next(slot)
+                    source(side), target(side), arrival.at[row, side], at(x, to_z, side), slots[side]
                 )
+
+        copies.group(home & wanted(to_z), across)
 
     def wanted(to_z):
         return (x < RING - 1) | (zhi == 0) | (lax.div(to_z, 2) == 1)
 
-    slots = [copies.slot() for _ in range(14)]
-    for m in range(1, pairs):
-        spread(
-            mine == m,
-            lambda side, m=m: fac.at[pl.ds(side * half, half), pl.ds(0, wide * m)],
-            lambda side, m=m: lbuf[m].at[pl.ds(aligned(odd * size + side * half, 8), half), :],
-            rl,
-            [(m // 2, x == m // 2)],
-            wanted,
+    def own_left(how, slots, numbers):
+        for m in numbers:
+            if m == 0:
+                continue
+            copies.group(
+                mine == m,
+                lambda m=m: how(
+                    lambda side: fac.at[pl.ds(side * half, half), pl.ds(0, wide * m)],
+                    lambda side: lbuf[m].at[pl.ds(aligned(odd * size + side * half, 8), half), :],
+                    rl,
+                    slots,
+                ),
+            )
+
+    def own_right(how, slots):
+        how(
+            lambda side: own.at[pl.ds(side * half, half), :],
+            lambda side: ebuf.at[pl.ds(aligned(row * size + side * half, 8), half), :],
+            re,
             slots,
         )
 
-    xa[...] = jnp.zeros_like(xa)
-    inverse = unit_lower_inverse(diag[...])
-    dinv[...] = inverse
-    beside = at(x, z + 1 - 2 * odd, core)
-    copies.remote(odd == 0, dinv, dleft, rd, beside)
+    slots = [copies.slot() for _ in range(8)]
+    own_left(near, slots, range(pairs))
+    farther = [copies.slot() for _ in range(4)]
+
     r_ids = lax.broadcasted_iota(jnp.int32, (size, wide), 0)
     c_ids = lax.broadcasted_iota(jnp.int32, (size, wide), 1)
     place = jnp.where(c_ids == r_ids + odd * size, 1.0, 0.0).astype(jnp.float32)
-    own[:, pl.ds(0, wide)] = dot(inverse, place)
+    own[:, pl.ds(0, wide)] = dot(dinv[...], place)
     own[:, pl.ds(wide, rhs.shape[1])] = rhs[...]
 
     @pl.when(odd == 1)
@@ -158,16 +211,8 @@
         lead = jnp.where(c_ids == r_ids, 1.0, 0.0).astype(jnp.float32)
         own[:, pl.ds(0, wide)] = own[:, pl.ds(0, wide)] - dot(left, lead)
 
-    slots = [copies.slot() for _ in range(14)]
-    spread(
-        mine >= 0,
-        lambda side: own.at[pl.ds(side * half, half), :],
-        lambda side: ebuf.at[pl.ds(aligned(row * size + side * half, 8), half), :],
-        re,
-        [(r, x == r) for r in range(RING)],
-        wanted,
-        slots,
-    )
+    slots = [copies.slot() for _ in range(8)]
+    own_right(near, slots)
 
     def view(kind, j, side):
         if kind == "left":
@@ -182,38 +227,73 @@
 
     def forward(kind, j, when, targets, beside_too):
         here, sem = view(kind, j, core), sem_of(kind, j, core)
-        arrived(when, here, sem)
-        for to_x in targets:
-            copies.remote(when, here, here, sem, at(to_x, z, core))
-        if beside_too is not None:
-            copies.remote(when & beside_too, here, here, sem, at(x, z, 1 - core))
-
-    for kind in ("left", "right"):
-        for r in range(RING):
-            for j in panels(kind, range(RING * r, RING * (r + 1))):
-                when = (x == r) & (z != j % RING)
-                if r == RING - 1 and j % RING >= 2:
-                    when = when & (zhi == 1)
-                forward(kind, j, when, TARGETS[r], mine >= j // 2)
-    for kind in ("left", "right"):
-        for r, targets in RELAYED.items():
-            for j in panels(kind, range(RING * r, RING * (r + 1))):
-                forward(kind, j, x == 0, targets, None)
+
+        def pass_on():
+            copies.arrived(here, sem)
+            for to_x in targets:
+                copies.remote(here, here, sem, at(to_x, z, core))
+            if beside_too is not None:
+                copies.group(
+                    beside_too, lambda: copies.remote(here, here, sem, at(x, z, 1 - core))
+                )
+
+        copies.group(when, pass_on)
+
+    def row_pass(kind, r, hops, targets, beside_too=True):
+        for j in panels(kind, range(RING * r, RING * (r + 1))):
+            apart = lax.rem(z + RING - j % RING, RING)
+            when = lax.rem(apart, 2) == 1 if hops == 1 else apart == hops
+            if r == RING - 1 and j % RING >= 2:
+                when = when & (zhi == 1)
+            forward(kind, j, when, targets, (mine >= j // 2) if beside_too else None)
+
+    for r in range(RING):
+
+        def own_row(r=r):
+            relays = [(kind, q, RELAYED[q]) for q in RELAYED for kind in ("left", "right") if r == 0]
+
+            def relay(kind, hops):
+                for name, q, targets in relays:
+                    if name == kind:
+                        row_pass(kind, q, hops, targets, False)
+
+            row_pass("left", r, 1, TARGETS[r])
+            own_left(far, farther[:2], (2 * r, 2 * r + 1))
+            relay("left", 0)
+            row_pass("right", r, 1, TARGETS[r])
+            own_right(far, farther[2:])
+            relay("left", 1)
+            row_pass("left", r, 2, TARGETS[r])
+            row_pass("right", r, 2, TARGETS[r])
+            relay("left", 2)
+            for hops in range(3):
+                relay("right", hops)
+
+        copies.group(x == r, own_row)
 
     def take(m):
-        for kind in ("left", "right"):
-            for j in panels(kind, (2 * m, 2 * m + 1)):
-                forward(kind, j, x > m // 2, (), mine >= 0)
+        def body():
+            for kind in ("left", "right"):
+                for j in panels(kind, (2 * m, 2 * m + 1)):
+                    forward(kind, j, True, (), True)
+
+        copies.group(x > m // 2, body)
 
     partner = at(x, z + 1 - 2 * odd, 1 - core)
     half_of_pair = jnp.where(home, odd, 1 - odd)
 
     def solve(m):
         here = mine >= m
-        for kind in ("left", "right"):
-            for j in panels(kind, (2 * m, 2 * m + 1)):
-                arrived(row == j, view(kind, j, core), sem_of(kind, j, core))
-                arrived(here, view(kind, j, 1 - core), sem_of(kind, j, 1 - core))
+
+        def wait():
+            for kind in ("left", "right"):
+                for j in panels(kind, (2 * m, 2 * m + 1)):
+                    pl.when(row == j)(
+                        lambda kind=kind, j=j: copies.arrived(view(kind, j, core), sem_of(kind, j, core))
+                    )
+                    copies.arrived(view(kind, j, 1 - core), sem_of(kind, j, 1 - core))
+
+        pl.when(here)(wait)
         block = xa.at[:, pl.ds(m * wide, wide)]
 
         @pl.when(mine == m)
@@ -222,36 +302,40 @@
 
         @pl.when(mine > m)
         def _():
-            block[...] = dot(block[...], ebuf[pl.ds(m * wide, wide), pl.ds(0, wide)])
+            block[...] = dot3(split(block[...]), split(ebuf[pl.ds(m * wide, wide), pl.ds(0, wide)]))
 
         @pl.when(here)
         def _():
-            dloc[...] += dot(block[...], ebuf[pl.ds(m * wide, wide), pl.ds(wide, dloc.shape[1])])
-
-        if m:
-
-            @pl.when(here)
-            def _():
+            solved = split(block[...])
+            dloc[...] += dot3(
+                solved, split(ebuf[pl.ds(m * wide, wide), pl.ds(wide, dloc.shape[1])])
+            )
+            parts[0, :, :], parts[1, :, :] = solved
+            if m:
+
                 @pl.loop(0, m)
                 def _(n):
                     cols = pl.ds(pl.multiple_of(n * wide, wide), wide)
-                    xa[:, cols] -= dot(block[...], lbuf[m][:, cols])
+                    xa[:, cols] -= dot3((parts[0], parts[1]), split(lbuf[m][:, cols]))
 
         result = inv.at[:, pl.ds(m * wide, wide)]
-        copies.local((mine < m) | home, block, result, lx.at[m])
-        copies.remote(here & away, block, result, rx.at[m], partner)
-
-    dloc[...] = jnp.zeros_like(dloc)
+        copies.group((mine < m) | home, lambda: copies.local(block, result, lx.at[m]))
+        copies.group(here & away, lambda: copies.remote(block, result, rx.at[m], partner))
+
     for m in reversed(range(pairs)):
         solve(m)
         if 2 <= m:
             take(m - 2)
-    copies.local(home, dloc, direct, lx.at[pairs])
-    copies.remote(away, dloc, direct, rx.at[pairs], partner)
-
-    for m in range(pairs):
-        arrived(away & (mine >= m), inv.at[:, pl.ds(m * wide, wide)], rx.at[m])
-    arrived(away, direct, rx.at[pairs])
+    copies.group(home, lambda: copies.local(dloc, direct, lx.at[pairs]))
+    copies.group(away, lambda: copies.remote(dloc, direct, rx.at[pairs], partner))
+
+    @pl.when(away)
+    def _():
+        for m in range(pairs):
+            result = inv.at[:, pl.ds(m * wide, wide)]
+            pl.when(mine >= m)(lambda m=m, result=result: copies.arrived(result, rx.at[m]))
+        copies.arrived(direct, rx.at[pairs])
+
     copies.finish()
 
 
@@ -282,7 +366,8 @@
             pltpu.VMEM((size, size), jnp.float32),
             pltpu.VMEM((size, size), jnp.float32),
             pltpu.VMEM((size, columns), jnp.float32),
-            dma((200,)),
+            pltpu.VMEM((2, size, wide), jnp.bfloat16),
+            dma((400,)),
             dma((panels, 2)),
             dma((panels, 2)),
             dma((pairs + 1,)),
@@ -332,12 +417,10 @@
         mapped[:, pl.ds(width, direct.shape[1])] = direct[pl.ds(size - width, width), :]
 
     for step in range(1, blocks):
-        copies.remote(
+        later = {"blk": lax.rem(blk + step, blocks), "row": row}
+        copies.group(
             last & (blk + step < blocks),
-            mapped,
-            maps.at[blk],
-            rm.at[blk],
-            {"blk": lax.rem(blk + step, blocks), "row": row},
+            lambda later=later: copies.remote(mapped, maps.at[blk], rm.at[blk], later),
         )
     for k in range(blocks - 1):
 
@@ -349,9 +432,12 @@
                 + maps[k, :, pl.ds(width, tail.shape[1])]
             )
 
-    for device in along:
-        copies.remote(last & (blk > 0), tail, tail, rt, device)
-    arrived((row != rows - 1) & (blk > 0), tail, rt)
+    def hand_out():
+        for device in along:
+            copies.remote(tail, tail, rt, device)
+
+    copies.group(last & (blk > 0), hand_out)
+    pl.when((row != rows - 1) & (blk > 0))(lambda: copies.arrived(tail, rt))
     out[...] = direct[...] + dot(gain[...], tail[...])
     copies.finish()
 

time: 172 us -> 149 us (0.87)
  the two profiles are of different devices: /device:TPU:29 before, /device:TPU:61 now
where the time goes in v2:
time: 149 us
  Pallas kernels  142 us (95%)
  local copies, waits for them, and re-layouts  5.83 us (4%)
    pallas_call x1, Pallas kernels, invert(): pl.pallas_call(functools.partial(solve_kernel, pairs), out_shape=(jax.Sha...  104 us
    pallas_call x1, Pallas kernels, chain(): pl.pallas_call(tail_kernel, out_shape=jax.ShapeDtypeStruct((size, columns...  37.9 us
    unnamed x10, local copies, waits for them, and re-layouts  4.6 us

profile of v2, /device:TPU:61, one launch (start us, length us, event | category | flops | bytes accessed | tf_op | source)
XLA Modules:
  0.0 148.8 jit_solution(14504920938426418687)
XLA Ops:
  0.6 0.0 copy-start.3
  0.7 1.2 dynamic-slice_bitcast_fusion
  1.9 0.0 copy-start.2
  1.9 0.9 copy-done.2
  2.8 104.3 %shard_map.50 = (f32[192,3072]{1,0:T(8,128)}, f32[192,128]{1,0:T(8,128)S(1)}) custom-call(f32[192,3072]{1,0:T(8,128)} %bitcast.13, f32[192,192]{1,0:T(8,128)S(1)} %get-tuple-element.7.diag, f32[192,192]{1,0:T(8,128)S(1)} %get-tuple-element.6.corner, f32[192,128]{1,0:T(8,128)S(1)} %bitcast.11), custom_call_target="tpu_custom_call" | custom-call | tf_op jit(solution)/shard_map/pallas_call | solution.py:353
  107.1 0.0 copy-done.3
  107.1 0.0 copy-start
  107.1 1.7 %copy-done = f32[192,3072]{1,0:T(8,128)S(1)} copy-done((f32[192,3072]{1,0:T(8,128)S(1)}, f32[192,3072]{1,0:T(8,128)}, u32[]{:S(2)}) %copy-start) | copy-done | bytes 2359320
  108.8 0.0 copy-start.1
  108.8 37.9 %shard_map.51 = f32[192,128]{1,0:T(8,128)S(1)} custom-call(f32[192,3072]{1,0:T(8,128)S(1)} %copy-done, f32[192,128]{1,0:T(8,128)S(1)} %get-tuple-element.5.direct, f32[128,128]{1,0:T(8,128)S(1)} %bitcast.12), custom_call_target="tpu_custom_call" | custom-call | tf_op jit(solution)/shard_map/pallas_call | solution.py:451
  146.7 0.0 copy-done.1
  146.7 1.4 copy.7
  148.1 0.6 copy.8
Async XLA Ops:
  0.6 106.5 %copy-start.3 = (f32[1,128,128]{2,1,0:T(8,128)S(1)}, f32[1,128,128]{2,1,0:T(8,128)}, u32[]{:S(2)}) copy-start(f32[1,128,128]{2,1,0:T(8,128)} %param.4) | copy-start | bytes 196612
  1.9 0.9 copy-start.2
  107.1 1.7 %copy-start = (f32[192,3072]{1,0:T(8,128)S(1)}, f32[192,3072]{1,0:T(8,128)}, u32[]{:S(2)}) copy-start(f32[192,3072]{1,0:T(8,128)} %get-tuple-element.4.inv) | copy-start | bytes 7077892
  108.8 37.9 %copy-start.1 = (f32[192,3072]{1,0:T(8,128)S(1)}, f32[192,3072]{1,0:T(8,128)}, u32[]{:S(2)}) copy-start(f32[192,3072]{1,0:T(8,128)} %get-tuple-element.4.inv) | copy-start | bytes 7077892

commit v3 on v2

--- a/solution.py
+++ b/solution.py
@@ -95,9 +95,12 @@
             self.group(when, body)
 
 
-def solve_kernel(pairs, fac, diag, corner, rhs, inv, direct, *scratch):
+def solve_kernel(pairs, planes, fac, diag, corner, rhs, coupling, inv, solved, *scratch):
     lbuf = (None, *scratch[: pairs - 1])
-    ebuf, own, xa, dinv, dleft, dloc, parts, sends, rl, re, rx, rd, lx = scratch[pairs - 1 :]
+    ebuf, own, xa, dinv, dleft, dloc, parts, cpl, gain, maps, mine_map, joined, tail = scratch[
+        pairs - 1 : pairs + 12
+    ]
+    sends, rl, re, rx, rd, lx, rc, rp, rj, rt = scratch[pairs + 12 :]
     size = fac.shape[0]
     half, wide = size // 2, 2 * size
     blk, row = lax.axis_index("blk"), lax.axis_index("row")
@@ -120,8 +123,12 @@
     for step in range(1, RING):
         for side in range(2):
             peers += [(x, lax.rem(z + step, RING), side), (lax.rem(x + step, RING), z, side)]
+    others = [
+        {"blk": lax.rem(blk + 2 * step, 2 * planes), "row": row} for step in range(1, planes)
+    ]
+    peers = [at(*peer) for peer in peers] + others
     for peer in peers:
-        pl.semaphore_signal(barrier, inc=1, device_id=at(*peer), device_id_type=MESH)
+        pl.semaphore_signal(barrier, inc=1, device_id=peer, device_id_type=MESH)
 
     xa[...] = jnp.zeros_like(xa)
     dloc[...] = jnp.zeros_like(dloc)
@@ -130,6 +137,12 @@
 
     copies = Copies(sends)
     beside = at(x, z + 1 - 2 * odd, core)
+
+    def share_coupling():
+        copies.local(coupling, cpl, rc, waited=False)
+        copies.remote(coupling, cpl, rc, at(x, z, 1 - core))
+
+    copies.group(home, share_coupling)
     copies.group(odd == 0, lambda: copies.remote(dinv, dleft, rd, beside))
 
     def near(source, target, arrival, slots):
@@ -281,6 +294,9 @@
 
     partner = at(x, z + 1 - 2 * odd, 1 - core)
     half_of_pair = jnp.where(home, odd, 1 - odd)
+    edge = RING - 1
+    row_lead = (zhi == 1) & (core == 0)
+    last = row_lead & (x == edge)
 
     def solve(m):
         here = mine >= m
@@ -320,28 +336,95 @@
 
         result = inv.at[:, pl.ds(m * wide, wide)]
         copies.group((mine < m) | home, lambda: copies.local(block, result, lx.at[m]))
-        copies.group(here & away, lambda: copies.remote(block, result, rx.at[m], partner))
+        when = here & away
+        if m < pairs // 2:
+            when = when & jnp.logical_not(last)
+        copies.group(when, lambda: copies.remote(block, result, rx.at[m], partner))
 
     for m in reversed(range(pairs)):
         solve(m)
         if 2 <= m:
             take(m - 2)
-    copies.group(home, lambda: copies.local(dloc, direct, lx.at[pairs]))
-    copies.group(away, lambda: copies.remote(dloc, direct, rx.at[pairs], partner))
+    width, columns = cpl.shape[0], dloc.shape[1]
+    plane, which = lax.div(blk, 2), 1 - odd
+    later = (plane > 0) | (which > 0)
+    copies.arrived(cpl, rc)
+    gain[...] = -dot(xa[:, pl.ds(0, width)], cpl[...])
+
+    @pl.when(last | jnp.logical_not(later))
+    def _():
+        tail[...] = jnp.zeros_like(tail)
+
+    @pl.when(last)
+    def _():
+        maps[which, :, pl.ds(0, width)] = gain[pl.ds(size - width, width), :]
+        maps[which, :, pl.ds(width, columns)] = dloc[pl.ds(size - width, width), :]
+
+    copies.group(last, lambda: copies.remote(maps.at[which], maps.at[which], rp, beside))
+
+    def held_back():
+        for m in reversed(range(pairs // 2)):
+            cols = pl.ds(m * wide, wide)
+            copies.remote(xa.at[:, cols], inv.at[:, cols], rx.at[m], partner)
+
+    copies.group(last & away, held_back)
+
+    @pl.when(last)
+    def _():
+        copies.arrived(maps.at[1 - which], rp)
+        mine_map[...] = dot(maps[1, :, pl.ds(0, width)], maps[0, :, :])
+        mine_map[:, pl.ds(width, columns)] += maps[1, :, pl.ds(width, columns)]
+
+    for step, device in enumerate(others):
+        copies.group(
+            last & (plane + step + 1 < planes),
+            lambda device=device: copies.remote(
+                mine_map, joined.at[plane], rj.at[plane], device
+            ),
+        )
+
+    def step_on(matrix_and_term):
+        left = matrix_and_term[:, pl.ds(0, width)]
+        tail[...] = dot(left, tail[...]) + matrix_and_term[:, pl.ds(width, columns)]
+
+    for k in range(planes - 1):
+
+        @pl.when(last & (plane > k))
+        def _():
+            copies.arrived(joined.at[k], rj.at[k])
+            step_on(joined.at[k])
+
+    @pl.when(last & (which == 1))
+    def _():
+        step_on(maps.at[0])
+
+    def hand_out(devices):
+        for device in devices:
+            copies.remote(tail, tail, rt, device)
+
+    pl.when(later & jnp.logical_not(last))(lambda: copies.arrived(tail, rt))
+    copies.group(later & last, lambda: hand_out([at(to_x, z, 0) for to_x in range(edge)]))
+    copies.group(
+        later & row_lead, lambda: hand_out([at(x, z - 2, 0), at(x, z - 2, 1), at(x, z, 1)])
+    )
+    dloc[...] += dot(gain[...], tail[...])
+    copies.group(home, lambda: copies.local(dloc, solved, lx.at[pairs]))
+    copies.group(away, lambda: copies.remote(dloc, solved, rx.at[pairs], partner))
 
     @pl.when(away)
     def _():
         for m in range(pairs):
             result = inv.at[:, pl.ds(m * wide, wide)]
             pl.when(mine >= m)(lambda m=m, result=result: copies.arrived(result, rx.at[m]))
-        copies.arrived(direct, rx.at[pairs])
+        copies.arrived(solved, rx.at[pairs])
 
     copies.finish()
 
 
-def invert(factor, right_side):
+def invert(factor, coupling, right_side):
     size, order = factor.shape
-    columns = right_side.shape[1]
+    columns, width = right_side.shape[1], coupling.shape[0]
+    planes = lax.axis_size("blk") // 2
     pairs, wide = order // (2 * size), 2 * size
     row = lax.axis_index("row")
     diag = lax.dynamic_slice_in_dim(factor, row * size, size, 1)
@@ -351,12 +434,12 @@
     dma = pltpu.SemaphoreType.DMA
     panels = 2 * pairs
     return pl.pallas_call(
-        functools.partial(solve_kernel, pairs),
+        functools.partial(solve_kernel, pairs, planes),
         out_shape=(
             jax.ShapeDtypeStruct((size, order), jnp.float32),
             jax.ShapeDtypeStruct((size, columns), jnp.float32),
         ),
-        in_specs=[vmem] * 4,
+        in_specs=[vmem] * 5,
         out_specs=(hbm, hbm),
         scratch_shapes=[
             *[pltpu.VMEM((wide, wide * m), jnp.float32) for m in range(1, pairs)],
@@ -367,112 +450,32 @@
             pltpu.VMEM((size, size), jnp.float32),
             pltpu.VMEM((size, columns), jnp.float32),
             pltpu.VMEM((2, size, wide), jnp.bfloat16),
+            pltpu.VMEM((width, width), jnp.float32),
+            pltpu.VMEM((size, width), jnp.float32),
+            pltpu.VMEM((2, width, width + columns), jnp.float32),
+            pltpu.VMEM((width, width + columns), jnp.float32),
+            pltpu.VMEM((planes, width, width + columns), jnp.float32),
+            pltpu.VMEM((width, columns), jnp.float32),
             dma((400,)),
             dma((panels, 2)),
             dma((panels, 2)),
             dma((pairs + 1,)),
             dma,
             dma((pairs + 1,)),
+            dma,
+            dma,
+            dma((planes,)),
+            dma,
         ],
         compiler_params=pltpu.CompilerParams(
             collective_id=0, has_side_effects=True, vmem_limit_bytes=52 * 1024 * 1024
         ),
-    )(factor, diag, corner, right_side)
-
-
-def tail_kernel(inv, direct, coupling, out, lead, gain, mapped, maps, tail, sends, rm, rt, lsem):
-    size, width = lead.shape
-    blocks, rows = maps.shape[0], lax.axis_size("row")
-    blk, row = lax.axis_index("blk"), lax.axis_index("row")
-    last = row == rows - 1
-    barrier = pltpu.get_barrier_semaphore()
-
-    def greet(when, device):
-        def _():
-            pl.semaphore_signal(barrier, inc=1, device_id=device, device_id_type=MESH)
-
-        pl.when(when)(_)
-
-    others = [{"blk": lax.rem(blk + step, blocks), "row": row} for step in range(1, blocks)]
-    along = [{"blk": blk, "row": number} for number in range(rows - 1)]
-    for device in others + along:
-        greet(last, device)
-    greet(row != rows - 1, {"blk": blk, "row": rows - 1})
-    pl.when(last)(lambda: pl.semaphore_wait(barrier, blocks + rows - 2))
-    pl.when(row != rows - 1)(lambda: pl.semaphore_wait(barrier, 1))
-
-    copies = Copies(sends)
-    fetch = pltpu.make_async_copy(inv.at[:, pl.ds(0, width)], lead, lsem)
-    fetch.start()
-    fetch.wait()
-    gain[...] = -dot(lead[...], coupling[...])
-
-    @pl.when(last | (blk == 0))
-    def _():
-        tail[...] = jnp.zeros_like(tail)
-
-    @pl.when(last)
-    def _():
-        mapped[:, pl.ds(0, width)] = gain[pl.ds(size - width, width), :]
-        mapped[:, pl.ds(width, direct.shape[1])] = direct[pl.ds(size - width, width), :]
-
-    for step in range(1, blocks):
-        later = {"blk": lax.rem(blk + step, blocks), "row": row}
-        copies.group(
-            last & (blk + step < blocks),
-            lambda later=later: copies.remote(mapped, maps.at[blk], rm.at[blk], later),
-        )
-    for k in range(blocks - 1):
-
-        @pl.when(last & (blk > k))
-        def _():
-            pltpu.make_async_copy(maps.at[k], maps.at[k], rm.at[k]).wait()
-            tail[...] = (
-                dot(maps[k, :, pl.ds(0, width)], tail[...])
-                + maps[k, :, pl.ds(width, tail.shape[1])]
-            )
-
-    def hand_out():
-        for device in along:
-            copies.remote(tail, tail, rt, device)
-
-    copies.group(last & (blk > 0), hand_out)
-    pl.when((row != rows - 1) & (blk > 0))(lambda: copies.arrived(tail, rt))
-    out[...] = direct[...] + dot(gain[...], tail[...])
-    copies.finish()
-
-
-def chain(inverse, direct, coupling):
-    size, columns = direct.shape
-    width = coupling.shape[0]
-    blocks, rows = lax.axis_size("blk"), lax.axis_size("row")
-    vmem = pl.BlockSpec(memory_space=pltpu.VMEM)
-    dma = pltpu.SemaphoreType.DMA
-    return pl.pallas_call(
-        tail_kernel,
-        out_shape=jax.ShapeDtypeStruct((size, columns), jnp.float32),
-        in_specs=[pl.BlockSpec(memory_space=pl.ANY), vmem, vmem],
-        out_specs=vmem,
-        scratch_shapes=[
-            pltpu.VMEM((size, width), jnp.float32),
-            pltpu.VMEM((size, width), jnp.float32),
-            pltpu.VMEM((width, width + columns), jnp.float32),
-            pltpu.VMEM((blocks, width, width + columns), jnp.float32),
-            pltpu.VMEM((width, columns), jnp.float32),
-            dma((blocks + rows,)),
-            dma((blocks,)),
-            dma,
-            dma,
-        ],
-        compiler_params=pltpu.CompilerParams(
-            collective_id=1, has_side_effects=True, vmem_limit_bytes=16 * 1024 * 1024
-        ),
-    )(inverse, direct, coupling)
+    )(factor, diag, corner, right_side, coupling)
 
 
 def on_device(factor, coupling, right_side):
-    inverse, direct = invert(factor[0], right_side[0])
-    return inverse[None], chain(inverse, direct, coupling[0])[None]
+    inverse, solved = invert(factor[0], coupling[0], right_side[0])
+    return inverse[None], solved[None]
 
 
 def solution(mesh):

time: 149 us -> 134 us (0.90)
  the two profiles are of different devices: /device:TPU:61 before, /device:TPU:49 now
where the time goes in v3:
time: 134 us
  Pallas kernels  126 us (94%)
  local copies, waits for them, and re-layouts  6.91 us (5%)
    pallas_call x1, Pallas kernels, invert(): pl.pallas_call(functools.partial(solve_kernel, pairs, planes), out_shape=...  126 us
    unnamed x6, local copies, waits for them, and re-layouts  5.67 us

profile of v3, /device:TPU:49, one launch (start us, length us, event | category | flops | bytes accessed | tf_op | source)
XLA Modules:
  0.0 133.8 jit_solution(9305292250872094996)
XLA Ops:
  0.6 1.2 dynamic-slice_bitcast_fusion
  1.9 0.0 copy-start
  1.9 0.9 copy-done
  2.8 0.0 copy-start.1
  2.8 0.8 copy-done.1
  3.6 126.2 %shard_map.50 = (f32[192,3072]{1,0:T(8,128)}, f32[192,128]{1,0:T(8,128)S(1)}) custom-call(f32[192,3072]{1,0:T(8,128)} %bitcast.12, f32[192,192]{1,0:T(8,128)S(1)} %get-tuple-element.7.diag, f32[192,192]{1,0:T(8,128)S(1)} %get-tuple-element.6.corner, f32[192,128]{1,0:T(8,128)S(1)} %bitcast.9, f32[128,128]{1,0:T(8,128)S(1)} %bitcast.11), custom_call_target="tpu_custom_call" | custom-call | tf_op jit(solution)/shard_map/pallas_call | solution.py:436
  129.8 3.3 %copy.7 = f32[1,192,3072]{2,1,0:T(8,128)} copy(f32[1,192,3072]{2,1,0:T(8,128)} %bitcast.13) | data formatting | bytes 4718592
  133.1 0.6 copy.8
Async XLA Ops:
  1.9 0.9 copy-start
  2.8 0.8 copy-start.1

commit v4 on v3

--- a/solution.py
+++ b/solution.py
@@ -10,6 +10,7 @@
 MESH = pl.DeviceIdType.MESH
 RING = 4
 TARGETS = {0: (3, 1, 2), 1: (0, 2), 2: (3,), 3: ()}
+TURNED = (2,)
 RELAYED = {1: (3,)}
 
 
@@ -95,7 +96,7 @@
             self.group(when, body)
 
 
-def solve_kernel(pairs, planes, fac, diag, corner, rhs, coupling, inv, solved, *scratch):
+def solve_kernel(pairs, planes, fac, rhs, coupling, inv, solved, *scratch):
     lbuf = (None, *scratch[: pairs - 1])
     ebuf, own, xa, dinv, dleft, dloc, parts, cpl, gain, maps, mine_map, joined, tail = scratch[
         pairs - 1 : pairs + 12
@@ -103,6 +104,8 @@
     sends, rl, re, rx, rd, lx, rc, rp, rj, rt = scratch[pairs + 12 :]
     size = fac.shape[0]
     half, wide = size // 2, 2 * size
+    lead, unit = rhs.shape[1], min(128, size)
+    widths = (lead + -(-size // unit) * unit, lead + wide)
     blk, row = lax.axis_index("blk"), lax.axis_index("row")
     core = lax.rem(blk, 2)
     x, z = lax.div(row, RING), lax.rem(row, RING)
@@ -130,10 +133,32 @@
     for peer in peers:
         pl.semaphore_signal(barrier, inc=1, device_id=peer, device_id_type=MESH)
 
+    edge = RING - 1
+    row_lead = (zhi == 1) & (core == 0)
+    last = row_lead & (x == edge)
+    led = (zhi == 0) & (core == 0) & (x != edge)
+    over = [at(to_x, lax.rem(z + 2, RING), 0) for to_x in range(edge)]
+
+    @pl.when(last)
+    def _():
+        for peer in over:
+            pl.semaphore_signal(barrier, inc=1, device_id=peer, device_id_type=MESH)
+
+    @pl.when(led)
+    def _():
+        lead_of = at(edge, lax.rem(z + 2, RING), 0)
+        pl.semaphore_signal(barrier, inc=1, device_id=lead_of, device_id_type=MESH)
+
     xa[...] = jnp.zeros_like(xa)
     dloc[...] = jnp.zeros_like(dloc)
-    dinv[...] = unit_lower_inverse(diag[...])
-    pl.semaphore_wait(barrier, len(peers))
+    for m in range(pairs):
+        rest = pl.ds(widths[0], widths[1] - widths[0])
+        ebuf[pl.ds(m * wide, size), rest] = jnp.zeros((size, widths[1] - widths[0]), jnp.float32)
+    frame = fac[:, pl.ds(aligned(mine * wide, wide), wide)]
+    turned = pltpu.roll(frame, size, 1)
+    dinv[...] = unit_lower_inverse(jnp.where(odd == 1, turned, frame)[:, :size])
+    extra = jnp.where(last, len(over), jnp.where(led, 1, 0))
+    pl.semaphore_wait(barrier, len(peers) + extra)
 
     copies = Copies(sends)
     beside = at(x, z + 1 - 2 * odd, core)
@@ -200,12 +225,17 @@
             )
 
     def own_right(how, slots):
-        how(
-            lambda side: own.at[pl.ds(side * half, half), :],
-            lambda side: ebuf.at[pl.ds(aligned(row * size + side * half, 8), half), :],
-            re,
-            slots,
-        )
+        for parity, width in enumerate(widths):
+            cols = pl.ds(0, width)
+            copies.group(
+                odd == parity,
+                lambda cols=cols: how(
+                    lambda side: own.at[pl.ds(side * half, half), cols],
+                    lambda side: ebuf.at[pl.ds(aligned(row * size + side * half, 8), half), cols],
+                    re,
+                    slots,
+                ),
+            )
 
     slots = [copies.slot() for _ in range(8)]
     own_left(near, slots, range(pairs))
@@ -214,15 +244,15 @@
     r_ids = lax.broadcasted_iota(jnp.int32, (size, wide), 0)
     c_ids = lax.broadcasted_iota(jnp.int32, (size, wide), 1)
     place = jnp.where(c_ids == r_ids + odd * size, 1.0, 0.0).astype(jnp.float32)
-    own[:, pl.ds(0, wide)] = dot(dinv[...], place)
-    own[:, pl.ds(wide, rhs.shape[1])] = rhs[...]
+    own[:, pl.ds(lead, wide)] = dot(dinv[...], place)
+    own[:, pl.ds(0, lead)] = rhs[...]
 
     @pl.when(odd == 1)
     def _():
         pltpu.make_async_copy(dleft, dleft, rd).wait()
-        left = dot(dinv[...], dot(corner[...], dleft[...]))
-        lead = jnp.where(c_ids == r_ids, 1.0, 0.0).astype(jnp.float32)
-        own[:, pl.ds(0, wide)] = own[:, pl.ds(0, wide)] - dot(left, lead)
+        left = dot(dinv[...], dot(fac[:, pl.ds(aligned(mine * wide, wide), wide)][:, :size], dleft[...]))
+        front = jnp.where(c_ids == r_ids, 1.0, 0.0).astype(jnp.float32)
+        own[:, pl.ds(lead, wide)] = own[:, pl.ds(lead, wide)] - dot(left, front)
 
     slots = [copies.slot() for _ in range(8)]
     own_right(near, slots)
@@ -230,7 +260,8 @@
     def view(kind, j, side):
         if kind == "left":
             return lbuf[j // 2].at[pl.ds(aligned((j % 2) * size + side * half, 8), half), :]
-        return ebuf.at[pl.ds(aligned(j * size + side * half, 8), half), :]
+        cols = pl.ds(0, widths[j % 2])
+        return ebuf.at[pl.ds(aligned(j * size + side * half, 8), half), cols]
 
     def sem_of(kind, j, side):
         return (rl if kind == "left" else re).at[j, side]
@@ -238,13 +269,15 @@
     def panels(kind, numbers):
         return [j for j in numbers if kind == "right" or j >= 2]
 
-    def forward(kind, j, when, targets, beside_too):
+    def forward(kind, j, when, targets, beside_too, across=False):
         here, sem = view(kind, j, core), sem_of(kind, j, core)
 
         def pass_on():
             copies.arrived(here, sem)
             for to_x in targets:
                 copies.remote(here, here, sem, at(to_x, z, core))
+            if across:
+                copies.remote(here, here, sem, at(x, lax.rem(z + 2, RING), core))
             if beside_too is not None:
                 copies.group(
                     beside_too, lambda: copies.remote(here, here, sem, at(x, z, 1 - core))
@@ -260,6 +293,12 @@
                 when = when & (zhi == 1)
             forward(kind, j, when, targets, (mine >= j // 2) if beside_too else None)
 
+    def turn(kind, r):
+        for q in TURNED:
+            if q + 1 == r:
+                for j in panels(kind, range(RING * q, RING * (q + 1))):
+                    forward(kind, j, z == j % RING, (), mine >= j // 2, across=True)
+
     for r in range(RING):
 
         def own_row(r=r):
@@ -272,12 +311,15 @@
 
             row_pass("left", r, 1, TARGETS[r])
             own_left(far, farther[:2], (2 * r, 2 * r + 1))
+            turn("left", r)
             relay("left", 0)
             row_pass("right", r, 1, TARGETS[r])
             own_right(far, farther[2:])
+            turn("right", r)
             relay("left", 1)
-            row_pass("left", r, 2, TARGETS[r])
-            row_pass("right", r, 2, TARGETS[r])
+            onward = () if r in TURNED else TARGETS[r]
+            row_pass("left", r, 2, onward)
+            row_pass("right", r, 2, onward)
             relay("left", 2)
             for hops in range(3):
                 relay("right", hops)
@@ -288,15 +330,13 @@
         def body():
             for kind in ("left", "right"):
                 for j in panels(kind, (2 * m, 2 * m + 1)):
-                    forward(kind, j, True, (), True)
+                    when = (z != j % RING) if m // 2 in TURNED else True
+                    forward(kind, j, when, (), True)
 
         copies.group(x > m // 2, body)
 
     partner = at(x, z + 1 - 2 * odd, 1 - core)
     half_of_pair = jnp.where(home, odd, 1 - odd)
-    edge = RING - 1
-    row_lead = (zhi == 1) & (core == 0)
-    last = row_lead & (x == edge)
 
     def solve(m):
         here = mine >= m
@@ -314,17 +354,18 @@
 
         @pl.when(mine == m)
         def _():
-            block[...] = ebuf[pl.ds(aligned(m * wide + half_of_pair * size, 8), size), pl.ds(0, wide)]
+            rows = pl.ds(aligned(m * wide + half_of_pair * size, 8), size)
+            block[...] = ebuf[rows, pl.ds(lead, wide)]
 
         @pl.when(mine > m)
         def _():
-            block[...] = dot3(split(block[...]), split(ebuf[pl.ds(m * wide, wide), pl.ds(0, wide)]))
+            block[...] = dot3(split(block[...]), split(ebuf[pl.ds(m * wide, wide), pl.ds(lead, wide)]))
 
         @pl.when(here)
         def _():
             solved = split(block[...])
             dloc[...] += dot3(
-                solved, split(ebuf[pl.ds(m * wide, wide), pl.ds(wide, dloc.shape[1])])
+                solved, split(ebuf[pl.ds(m * wide, wide), pl.ds(0, lead)])
             )
             parts[0, :, :], parts[1, :, :] = solved
             if m:
@@ -403,9 +444,13 @@
             copies.remote(tail, tail, rt, device)
 
     pl.when(later & jnp.logical_not(last))(lambda: copies.arrived(tail, rt))
-    copies.group(later & last, lambda: hand_out([at(to_x, z, 0) for to_x in range(edge)]))
+    ahead = [at(to_x, z, 0) for to_x in range(edge)]
+    copies.group(later & last, lambda: hand_out([over[0], *ahead, *over[1:], at(x, z, 1)]))
     copies.group(
-        later & row_lead, lambda: hand_out([at(x, z - 2, 0), at(x, z - 2, 1), at(x, z, 1)])
+        later & led & (x == 0), lambda: hand_out([at(edge, z, 0), at(edge, z, 1)])
+    )
+    copies.group(
+        later & (core == 0) & (x != edge), lambda: hand_out([at(x, z, 1)])
     )
     dloc[...] += dot(gain[...], tail[...])
     copies.group(home, lambda: copies.local(dloc, solved, lx.at[pairs]))
@@ -426,9 +471,6 @@
     columns, width = right_side.shape[1], coupling.shape[0]
     planes = lax.axis_size("blk") // 2
     pairs, wide = order // (2 * size), 2 * size
-    row = lax.axis_index("row")
-    diag = lax.dynamic_slice_in_dim(factor, row * size, size, 1)
-    corner = lax.dynamic_slice_in_dim(factor, (row - row % 2) * size, size, 1)
     vmem = pl.BlockSpec(memory_space=pltpu.VMEM)
     hbm = pl.BlockSpec(memory_space=pl.ANY)
     dma = pltpu.SemaphoreType.DMA
@@ -439,7 +481,7 @@
             jax.ShapeDtypeStruct((size, order), jnp.float32),
             jax.ShapeDtypeStruct((size, columns), jnp.float32),
         ),
-        in_specs=[vmem] * 5,
+        in_specs=[vmem] * 3,
         out_specs=(hbm, hbm),
         scratch_shapes=[
             *[pltpu.VMEM((wide, wide * m), jnp.float32) for m in range(1, pairs)],
@@ -470,7 +512,7 @@
         compiler_params=pltpu.CompilerParams(
             collective_id=0, has_side_effects=True, vmem_limit_bytes=52 * 1024 * 1024
         ),
-    )(factor, diag, corner, right_side, coupling)
+    )(factor, right_side, coupling)
 
 
 def on_device(factor, coupling, right_side):

time: 134 us -> 130 us (0.970)
  the two profiles are of different devices: /device:TPU:49 before, /device:TPU:22 now
where the time goes in v4:
time: 130 us; the launch traced here: 129 us
  Pallas kernels  123 us (95%)
  local copies, waits for them, and re-layouts  5.66 us (4%)
    pallas_call x1, Pallas kernels, invert(): pl.pallas_call(functools.partial(solve_kernel, pairs, planes), out_shape=...  123 us
    unnamed x6, local copies, waits for them, and re-layouts  5.66 us

profile of v4, /device:TPU:22, one launch (start us, length us, event | category | flops | bytes accessed | tf_op | source)
XLA Modules:
  0.0 129.3 jit_solution(13749992316130877199)
XLA Ops:
  0.6 0.0 copy-start
  0.6 0.9 copy-done
  1.5 0.0 copy-start.1
  1.5 0.8 copy-done.1
  2.4 123.0 %shard_map.50 = (f32[192,3072]{1,0:T(8,128)}, f32[192,128]{1,0:T(8,128)S(1)}) custom-call(f32[192,3072]{1,0:T(8,128)} %bitcast.8, f32[192,128]{1,0:T(8,128)S(1)} %bitcast.5, f32[128,128]{1,0:T(8,128)S(1)} %bitcast.7), custom_call_target="tpu_custom_call" | custom-call | tf_op jit(solution)/shard_map/pallas_call | solution.py:478
  125.4 3.3 %copy.7 = f32[1,192,3072]{2,1,0:T(8,128)} copy(f32[1,192,3072]{2,1,0:T(8,128)} %bitcast.9) | data formatting | bytes 4718592
  128.7 0.6 copy.8
Async XLA Ops:
  0.6 0.9 copy-start
  1.5 0.8 copy-start.1

commit v5 on v4

--- a/solution.py
+++ b/solution.py
@@ -98,10 +98,10 @@
 
 def solve_kernel(pairs, planes, fac, rhs, coupling, inv, solved, *scratch):
     lbuf = (None, *scratch[: pairs - 1])
-    ebuf, own, xa, dinv, dleft, dloc, parts, cpl, gain, maps, mine_map, joined, tail = scratch[
-        pairs - 1 : pairs + 12
+    ebuf, own, xa, dinv, dleft, dloc, parts, cpl, gain, maps, mine_map, joined, tail, frames = scratch[
+        pairs - 1 : pairs + 13
     ]
-    sends, rl, re, rx, rd, lx, rc, rp, rj, rt = scratch[pairs + 12 :]
+    sends, rl, re, rx, rd, lx, rc, rp, rj, rt, lf = scratch[pairs + 13 :]
     size = fac.shape[0]
     half, wide = size // 2, 2 * size
     lead, unit = rhs.shape[1], min(128, size)
@@ -154,7 +154,10 @@
     for m in range(pairs):
         rest = pl.ds(widths[0], widths[1] - widths[0])
         ebuf[pl.ds(m * wide, size), rest] = jnp.zeros((size, widths[1] - widths[0]), jnp.float32)
-    frame = fac[:, pl.ds(aligned(mine * wide, wide), wide)]
+    part_of = pltpu.make_async_copy(fac.at[:, pl.ds(aligned(mine * wide, wide), wide)], frames, lf)
+    part_of.start()
+    part_of.wait()
+    frame = frames[...]
     turned = pltpu.roll(frame, size, 1)
     dinv[...] = unit_lower_inverse(jnp.where(odd == 1, turned, frame)[:, :size])
     extra = jnp.where(last, len(over), jnp.where(led, 1, 0))
@@ -250,7 +253,7 @@
     @pl.when(odd == 1)
     def _():
         pltpu.make_async_copy(dleft, dleft, rd).wait()
-        left = dot(dinv[...], dot(fac[:, pl.ds(aligned(mine * wide, wide), wide)][:, :size], dleft[...]))
+        left = dot(dinv[...], dot(frames[:, :size], dleft[...]))
         front = jnp.where(c_ids == r_ids, 1.0, 0.0).astype(jnp.float32)
         own[:, pl.ds(lead, wide)] = own[:, pl.ds(lead, wide)] - dot(left, front)
 
@@ -390,7 +393,7 @@
     plane, which = lax.div(blk, 2), 1 - odd
     later = (plane > 0) | (which > 0)
     copies.arrived(cpl, rc)
-    gain[...] = -dot(xa[:, pl.ds(0, width)], cpl[...])
+    gain[...] = -dot3(split(xa[:, pl.ds(0, width)]), split(cpl[...]))
 
     @pl.when(last | jnp.logical_not(later))
     def _():
@@ -413,7 +416,7 @@
     @pl.when(last)
     def _():
         copies.arrived(maps.at[1 - which], rp)
-        mine_map[...] = dot(maps[1, :, pl.ds(0, width)], maps[0, :, :])
+        mine_map[...] = dot3(split(maps[1, :, pl.ds(0, width)]), split(maps[0, :, :]))
         mine_map[:, pl.ds(width, columns)] += maps[1, :, pl.ds(width, columns)]
 
     for step, device in enumerate(others):
@@ -426,7 +429,7 @@
 
     def step_on(matrix_and_term):
         left = matrix_and_term[:, pl.ds(0, width)]
-        tail[...] = dot(left, tail[...]) + matrix_and_term[:, pl.ds(width, columns)]
+        tail[...] = dot3(split(left), split(tail[...])) + matrix_and_term[:, pl.ds(width, columns)]
 
     for k in range(planes - 1):
 
@@ -452,7 +455,7 @@
     copies.group(
         later & (core == 0) & (x != edge), lambda: hand_out([at(x, z, 1)])
     )
-    dloc[...] += dot(gain[...], tail[...])
+    dloc[...] += dot3(split(gain[...]), split(tail[...]))
     copies.group(home, lambda: copies.local(dloc, solved, lx.at[pairs]))
     copies.group(away, lambda: copies.remote(dloc, solved, rx.at[pairs], partner))
 
@@ -481,7 +484,7 @@
             jax.ShapeDtypeStruct((size, order), jnp.float32),
             jax.ShapeDtypeStruct((size, columns), jnp.float32),
         ),
-        in_specs=[vmem] * 3,
+        in_specs=[hbm, vmem, vmem],
         out_specs=(hbm, hbm),
         scratch_shapes=[
             *[pltpu.VMEM((wide, wide * m), jnp.float32) for m in range(1, pairs)],
@@ -498,6 +501,7 @@
             pltpu.VMEM((width, width + columns), jnp.float32),
             pltpu.VMEM((planes, width, width + columns), jnp.float32),
             pltpu.VMEM((width, columns), jnp.float32),
+            pltpu.VMEM((size, wide), jnp.float32),
             dma((400,)),
             dma((panels, 2)),
             dma((panels, 2)),
@@ -508,6 +512,7 @@
             dma,
             dma((planes,)),
             dma,
+            dma,
         ],
         compiler_params=pltpu.CompilerParams(
             collective_id=0, has_side_effects=True, vmem_limit_bytes=52 * 1024 * 1024

time: 130 us -> 129 us (level)
  no operation moved by 1% of the time
where the time goes in v5:
time: 129 us; the launch traced here: 128 us
  Pallas kernels  122 us (95%)
  local copies, waits for them, and re-layouts  5.66 us (4%)
    pallas_call x1, Pallas kernels, invert(): pl.pallas_call(functools.partial(solve_kernel, pairs, planes), out_shape=...  122 us
    unnamed x6, local copies, waits for them, and re-layouts  5.66 us

profile of v5, /device:TPU:22, one launch (start us, length us, event | category | flops | bytes accessed | tf_op | source)
XLA Modules:
  0.0 128.4 jit_solution(11385331154248330535)
XLA Ops:
  0.6 0.0 copy-start
  0.6 0.9 copy-done
  1.5 0.0 copy-start.1
  1.5 0.8 copy-done.1
  2.4 122.1 %shard_map.50 = (f32[192,3072]{1,0:T(8,128)}, f32[192,128]{1,0:T(8,128)S(1)}) custom-call(f32[192,3072]{1,0:T(8,128)} %bitcast.8, f32[192,128]{1,0:T(8,128)S(1)} %bitcast.5, f32[128,128]{1,0:T(8,128)S(1)} %bitcast.7), custom_call_target="tpu_custom_call" | custom-call | tf_op jit(solution)/shard_map/pallas_call | solution.py:481
  124.5 3.3 %copy.7 = f32[1,192,3072]{2,1,0:T(8,128)} copy(f32[1,192,3072]{2,1,0:T(8,128)} %bitcast.9) | data formatting | bytes 4718592
  127.8 0.6 copy.8
Async XLA Ops:
  0.6 0.9 copy-start
  1.5 0.8 copy-start.1

commit v6 on v5

--- a/solution.py
+++ b/solution.py
@@ -160,6 +160,12 @@
     frame = frames[...]
     turned = pltpu.roll(frame, size, 1)
     dinv[...] = unit_lower_inverse(jnp.where(odd == 1, turned, frame)[:, :size])
+    r_ids = lax.broadcasted_iota(jnp.int32, (size, wide), 0)
+    c_ids = lax.broadcasted_iota(jnp.int32, (size, wide), 1)
+    place = jnp.where(c_ids == r_ids + odd * size, 1.0, 0.0).astype(jnp.float32)
+    own[:, pl.ds(lead, wide)] = dot(dinv[...], place)
+    own[:, pl.ds(0, lead)] = rhs[...]
+    before = dot(dinv[...], frames[:, :size])
     extra = jnp.where(last, len(over), jnp.where(led, 1, 0))
     pl.semaphore_wait(barrier, len(peers) + extra)
 
@@ -244,16 +250,10 @@
     own_left(near, slots, range(pairs))
     farther = [copies.slot() for _ in range(4)]
 
-    r_ids = lax.broadcasted_iota(jnp.int32, (size, wide), 0)
-    c_ids = lax.broadcasted_iota(jnp.int32, (size, wide), 1)
-    place = jnp.where(c_ids == r_ids + odd * size, 1.0, 0.0).astype(jnp.float32)
-    own[:, pl.ds(lead, wide)] = dot(dinv[...], place)
-    own[:, pl.ds(0, lead)] = rhs[...]
-
     @pl.when(odd == 1)
     def _():
         pltpu.make_async_copy(dleft, dleft, rd).wait()
-        left = dot(dinv[...], dot(frames[:, :size], dleft[...]))
+        left = dot(before, dleft[...])
         front = jnp.where(c_ids == r_ids, 1.0, 0.0).astype(jnp.float32)
         own[:, pl.ds(lead, wide)] = own[:, pl.ds(lead, wide)] - dot(left, front)
 

time: 129 us -> 129 us (level)
  no operation moved by 1% of the time
where the time goes in v6:
time: 129 us
  Pallas kernels  123 us (95%)
  local copies, waits for them, and re-layouts  5.66 us (4%)
    pallas_call x1, Pallas kernels, invert(): pl.pallas_call(functools.partial(solve_kernel, pairs, planes), out_shape=...  123 us
    unnamed x6, local copies, waits for them, and re-layouts  5.66 us

profile of v6, /device:TPU:22, one launch (start us, length us, event | category | flops | bytes accessed | tf_op | source)
XLA Modules:
  0.0 129.0 jit_solution(1782168627093644048)
XLA Ops:
  0.6 0.0 copy-start
  0.6 0.9 copy-done
  1.5 0.0 copy-start.1
  1.5 0.8 copy-done.1
  2.4 122.7 %shard_map.50 = (f32[192,3072]{1,0:T(8,128)}, f32[192,128]{1,0:T(8,128)S(1)}) custom-call(f32[192,3072]{1,0:T(8,128)} %bitcast.8, f32[192,128]{1,0:T(8,128)S(1)} %bitcast.5, f32[128,128]{1,0:T(8,128)S(1)} %bitcast.7), custom_call_target="tpu_custom_call" | custom-call | tf_op jit(solution)/shard_map/pallas_call | solution.py:481
  125.0 3.3 %copy.7 = f32[1,192,3072]{2,1,0:T(8,128)} copy(f32[1,192,3072]{2,1,0:T(8,128)} %bitcast.9) | data formatting | bytes 4718592
  128.3 0.6 copy.8
Async XLA Ops:
  0.6 0.9 copy-start
  1.5 0.8 copy-start.1
